TPU v7x, 32 devices: a whole 2x2x4 slice. The times are simulated.
32 devices in a mesh: groups: 2 (over y), ctx: 4 (over z), head: 4 (over x, core).
Axes of the slice: x: 2, y: 2, z: 4, core: 2. Of those that a mesh axis runs over, the one named last changes fastest.
Arguments:
- queries: bfloat16 [2, 512, 4096], P(None, ('groups', 'ctx'), 'head'), parts along dimension 1, may hold values from -8 to 8
- keys: bfloat16 [2, 512, 1024], P(None, ('groups', 'ctx'), 'head'), parts along dimension 1, may hold values from -8 to 8
- values: bfloat16 [2, 512, 1024], P(None, ('groups', 'ctx'), 'head'), parts along dimension 1, may hold values from -6 to 6
- residual: bfloat16 [2, 512, 4096], P(None, ('groups', 'ctx'), 'head'), parts along dimension 1, may hold values from -6 to 6
- targets: bfloat16 [2, 512, 4096], P(None, ('groups', 'ctx'), 'head'), parts along dimension 1, may hold values from -6 to 6
- lang_ids: int32 [2, 512], P(None, ('groups', 'ctx')), parts along dimension 1, may hold values from 0 to 15
- lang_scale: float32 [16, 4096], P(None, 'head'), may hold values from 0.25 to 2
- out_weight: bfloat16 [4096, 4096], P('head'), may hold values from -0.09375 to 0.09375
Outputs:
- grad_queries: float32 [2, 512, 4096], P(None, ('groups', 'ctx'), 'head'), parts along dimension 1
- grad_keys: float32 [2, 512, 1024], P(None, ('groups', 'ctx'), 'head'), parts along dimension 1
- grad_values: float32 [2, 512, 1024], P(None, ('groups', 'ctx'), 'head'), parts along dimension 1
There are 2 independent parts, one for each index of `groups`. A program takes and returns all parts, laid end to end along the dimension named above; an argument that names none is the same for every part. Nothing has to cross between parts.
All inputs are finite; a program needn't handle non-finite values.
Results may differ from a plain program's by a relative error of at most 0.0062.
Values may be sent and summed in bfloat16 or wider, within the bound.
No kernel may reach another device: no remote copies, remote signals or barrier semaphores. Data moves between devices by JAX's collectives and lax.ppermute only.
A program may use at most 64 MiB of HBM per device.

v0:
```python
import jax
import jax.numpy as jnp
from jax import lax
from jax.sharding import PartitionSpec as P

HEAD_DIM = 128


BIG_NEG = -1e30


def passed_along(value, axis, steps):
    count = lax.axis_size(axis)
    pairs = [(source, (source + steps) % count) for source in range(count)]
    return lax.ppermute(value, axis, pairs)


def partner(block, axis, apart):
    count = lax.axis_size(axis)
    route = []
    for low in range(count):
        high = low | 1 << apart
        if high != low and high < count:
            route += [(low, high), (high, low)]
    return lax.ppermute(block, axis, route)


def span_positions(owner, span_rows, cycle_size, upper):
    offsets = jnp.arange(span_rows, dtype=jnp.int32)
    if upper:
        return (2 * cycle_size - 1 - owner) * span_rows + offsets
    return owner * span_rows + offsets


def attend(state, query_rows, query_pos, key_rows, value_rows, key_pos, score_scale):
    running_max, row_total, weighted = state
    scores = (
        jnp.einsum("rkgd,pkd->kgrp", query_rows, key_rows, preferred_element_type=jnp.float32)
        * score_scale
    )
    allowed = key_pos[None, :] <= query_pos[:, None]
    masked = jnp.where(allowed, scores, BIG_NEG)
    new_max = jnp.maximum(running_max, jnp.max(masked, axis=-1))
    weights = jnp.where(allowed, jnp.exp(masked - new_max[..., None]), 0.0)
    factor = jnp.exp(running_max - new_max)
    row_total = row_total * factor + jnp.sum(weights, axis=-1)
    weighted = weighted * factor[..., None] + jnp.einsum(
        "kgrp,pkd->kgrd", weights, value_rows.astype(jnp.float32), precision=lax.Precision.HIGHEST
    )
    return (new_max, row_total, weighted)


def attend_grad(
    grads,
    query_rows,
    grad_rows,
    log_norm,
    delta,
    query_pos,
    key_rows,
    value_rows,
    key_pos,
    score_scale,
):
    query_grad, key_grad, value_grad = grads
    scores = (
        jnp.einsum("rkgd,pkd->kgrp", query_rows, key_rows, preferred_element_type=jnp.float32)
        * score_scale
    )
    allowed = key_pos[None, :] <= query_pos[:, None]
    probs = jnp.exp(jnp.where(allowed, scores - log_norm[..., None], -jnp.inf))
    value_grad = value_grad + jnp.einsum(
        "kgrp,rkgd->pkd", probs.astype(jnp.bfloat16), grad_rows, preferred_element_type=jnp.float32
    )
    grad_prob = jnp.einsum(
        "rkgd,pkd->kgrp", grad_rows, value_rows, preferred_element_type=jnp.float32
    )
    grad_scores = (probs * (grad_prob - delta[..., None])).astype(jnp.bfloat16)
    query_grad = (
        query_grad
        + jnp.einsum("kgrp,pkd->rkgd", grad_scores, key_rows, preferred_element_type=jnp.float32)
        * score_scale
    )
    key_grad = (
        key_grad
        + jnp.einsum("kgrp,rkgd->pkd", grad_scores, query_rows, preferred_element_type=jnp.float32)
        * score_scale
    )
    return (query_grad, key_grad, value_grad)


def on_device(queries, keys, values, residual, targets, lang_ids, lang_scale, out_weight):
    cycle_size = lax.axis_size("ctx")
    device = lax.axis_index("ctx")
    span_rows = queries.shape[1]
    kv_local = keys.shape[2] // HEAD_DIM
    q_local = queries.shape[2] // HEAD_DIM
    per_group = q_local // kv_local
    score_scale = HEAD_DIM ** (-0.5)
    query_all = queries.reshape(2, span_rows, kv_local, per_group, HEAD_DIM)
    key_all = keys.reshape(2, span_rows, kv_local, HEAD_DIM)
    value_all = values.reshape(2, span_rows, kv_local, HEAD_DIM)
    query_pos = (
        span_positions(device, span_rows, cycle_size, False),
        span_positions(device, span_rows, cycle_size, True),
    )

    def forward_step(states, key_block, value_block, low_owner, high_owner):
        key_pos = (
            span_positions(low_owner, span_rows, cycle_size, False),
            span_positions(high_owner, span_rows, cycle_size, True),
        )

        def tile(state, query_half, key_half):
            return attend(
                state,
                query_all[query_half],
                query_pos[query_half],
                key_block[key_half],
                value_block[key_half],
                key_pos[key_half],
                score_scale,
            )

        low_state, high_state = states
        high_state = tile(high_state, 1, 0)
        low_state = tile(low_state, 0, 0)
        low_state = tile(low_state, 0, 1)
        high_state = tile(high_state, 1, 1)
        return (low_state, high_state)

    start_state = (
        jnp.full((kv_local, per_group, span_rows), BIG_NEG, jnp.float32),
        jnp.zeros((kv_local, per_group, span_rows), jnp.float32),
        jnp.zeros((kv_local, per_group, span_rows, HEAD_DIM), jnp.float32),
    )
    states = forward_step((start_state, start_state), key_all, value_all, device, device)

    def forward_turn(turn_index, loop_state):
        states, key_block, value_block = loop_state
        key_block, value_block = passed_along((key_block, value_block), "ctx", 1)
        source = (device - turn_index) % cycle_size
        states = forward_step(states, key_block, value_block, source, source)
        return (states, key_block, value_block)

    states, _, _ = lax.fori_loop(1, cycle_size, forward_turn, (states, key_all, value_all))

    def finish(state):
        running_max, row_total, weighted = state
        mixed = (weighted / row_total[..., None]).astype(jnp.bfloat16)
        return (mixed.transpose(2, 0, 1, 3), running_max + jnp.log(row_total))

    low_out, low_norm = finish(states[0])
    high_out, high_norm = finish(states[1])
    attended = jnp.stack([low_out, high_out])
    log_norms = jnp.stack([low_norm, high_norm])
    flat_attn = attended.reshape(2 * span_rows, q_local * HEAD_DIM)
    partial_proj = jnp.dot(flat_attn, out_weight, preferred_element_type=jnp.float32)
    projected = lax.psum_scatter(partial_proj, "head", scatter_dimension=1, tiled=True)
    width_local = projected.shape[1]
    languages = lang_ids.reshape(2 * span_rows)
    one_hot = (
        languages[:, None] == jnp.arange(lang_scale.shape[0], dtype=jnp.int32)[None, :]
    ).astype(jnp.float32)
    row_scales = jnp.dot(one_hot, lang_scale, precision=lax.Precision.HIGHEST)
    hidden = (
        residual.reshape(2 * span_rows, width_local).astype(jnp.float32) + projected * row_scales
    )
    upper_targets = targets[1]
    for bit_index in range(cycle_size.bit_length() - 1):
        upper_targets = partner(upper_targets, "ctx", bit_index)
    wanted = jnp.concatenate([targets[0], upper_targets]).astype(jnp.float32)
    grad_proj = ((hidden - wanted) * row_scales).astype(jnp.bfloat16)
    grad_attn = lax.dot_general(
        lax.all_gather(grad_proj, "head", axis=1, tiled=True),
        out_weight,
        (((1,), (1,)), ((), ())),
        preferred_element_type=jnp.float32,
    ).astype(jnp.bfloat16)
    grad_out = grad_attn.reshape(2, span_rows, kv_local, per_group, HEAD_DIM)
    deltas = jnp.sum(
        grad_out.astype(jnp.float32) * attended.astype(jnp.float32), axis=-1
    ).transpose(0, 2, 3, 1)

    def backward_step(grad_state, key_block, value_block, low_owner, high_owner):
        query_grads, key_grads, value_grads = grad_state
        key_pos = (
            span_positions(low_owner, span_rows, cycle_size, False),
            span_positions(high_owner, span_rows, cycle_size, True),
        )

        def tile(grads, query_half, key_half):
            return attend_grad(
                grads,
                query_all[query_half],
                grad_out[query_half],
                log_norms[query_half],
                deltas[query_half],
                query_pos[query_half],
                key_block[key_half],
                value_block[key_half],
                key_pos[key_half],
                score_scale,
            )

        low_query, high_query = query_grads
        low_key, high_key = (key_grads[0], key_grads[1])
        low_value, high_value = (value_grads[0], value_grads[1])
        high_query, low_key, low_value = tile((high_query, low_key, low_value), 1, 0)
        low_query, low_key, low_value = tile((low_query, low_key, low_value), 0, 0)
        low_query, high_key, high_value = tile((low_query, high_key, high_value), 0, 1)
        high_query, high_key, high_value = tile((high_query, high_key, high_value), 1, 1)
        return (
            (low_query, high_query),
            jnp.stack([low_key, high_key]),
            jnp.stack([low_value, high_value]),
        )

    zero_query = jnp.zeros((span_rows, kv_local, per_group, HEAD_DIM), jnp.float32)
    zero_keys = jnp.zeros((2, span_rows, kv_local, HEAD_DIM), jnp.float32)

    def backward_turn(turn_index, loop_state):
        query_grads, key_block, value_block, key_grads, value_grads = loop_state
        source = (device - turn_index) % cycle_size
        query_grads, key_grads, value_grads = backward_step(
            (query_grads, key_grads, value_grads), key_block, value_block, source, source
        )
        key_block, value_block = passed_along((key_block, value_block), "ctx", 1)
        key_grads, value_grads = passed_along((key_grads, value_grads), "ctx", 1)
        return (query_grads, key_block, value_block, key_grads, value_grads)

    final_state = lax.fori_loop(
        0,
        cycle_size,
        backward_turn,
        ((zero_query, zero_query), key_all, value_all, zero_keys, zero_keys),
    )
    query_grads, _, _, key_grads, value_grads = final_state
    grad_queries = jnp.stack(query_grads).reshape(2, span_rows, q_local * HEAD_DIM)
    grad_keys = key_grads.reshape(2, span_rows, kv_local * HEAD_DIM)
    grad_values = value_grads.reshape(2, span_rows, kv_local * HEAD_DIM)
    return (grad_queries, grad_keys, grad_values)


def solution(mesh):
    in_specs = (
        P(None, ("groups", "ctx"), "head"),
        P(None, ("groups", "ctx"), "head"),
        P(None, ("groups", "ctx"), "head"),
        P(None, ("groups", "ctx"), "head"),
        P(None, ("groups", "ctx"), "head"),
        P(None, ("groups", "ctx")),
        P(None, "head"),
        P("head", None),
    )
    out_specs = (
        P(None, ("groups", "ctx"), "head"),
        P(None, ("groups", "ctx"), "head"),
        P(None, ("groups", "ctx"), "head"),
    )
    return jax.shard_map(
        on_device, mesh=mesh, in_specs=in_specs, out_specs=out_specs, check_vma=False
    )
```

profile of v0, /device:TPU:0, one launch (start us, length us, event | category | flops | bytes accessed | tf_op | source)
XLA Modules:
  0.0 174.3 jit_solution(10340567299591559284)
XLA Ops:
  15.4 30.1 %while.56 = (s32[]{:T(128)}, f32[2,4,64]{2,1,0:T(4,128)S(1)}, f32[2,4,64]{2,1,0:T(4,128)S(1)}, f32[2,4,64,128]{3,2,1,0:T(8,128)S(1)}, f32[2,4,64]{2,1,0:T(4,128)...) while((s32[]{:T(128)}, f32[2,4,64]{2,1,0:T(4,128)S(1)}, ...), condition=%wide.region_17.18_spmd.clone, body=%wide.region_8.17_spmd.clone.sunk | while | flops 236474640 | bytes 5990826 | solution.py:146
  15.4 3.1 %collective-permute-start = (bf16[2,64,2,128]{3,1,2,0:T(8,128)(2,1)S(1)}, bf16[2,64,2,128]{3,1,2,0:T(8,128)(2,1)S(1)}, u32[]{:S(2)}, u32[]{:S(2)}) collective-permute-start(bf16[2,64,2,128]{3,1,2,0:T(8,128)(2,1)S(1)} %get-tuple-element.1218), channel_id=1, source_target_pairs={{0,4},{4,8},{8,12},{12,0},{1,5},{5,9},{9,13},{13,1},{2,6},{6,10},{... | collective-permute-start | bytes 196616 | tf_op jit(solution)/shard_map/while/body/eval_jaxpr/ppermute | solution.py:15
  18.5 1.6 collective-permute-start.1
  20.2 3.0 %collective-permute-done = bf16[2,64,2,128]{3,1,2,0:T(8,128)(2,1)S(1)} collective-permute-done((bf16[2,64,2,128]{3,1,2,0:T(8,128)(2,1)S(1)}, bf16[2,64,2,128]{3,1,2,0:T(8,128)(2,1)S(1)}, u32[]{:S(2)}, u32[]{:S(2)}) %collective-permute-start) | collective-permute-done | bytes 65568 | tf_op jit(solution)/shard_map/while/body/eval_jaxpr/ppermute | solution.py:15
  26.7 1.6 collective-permute-start.1
  28.4 4.2 %collective-permute-done = bf16[2,64,2,128]{3,1,2,0:T(8,128)(2,1)S(1)} collective-permute-done((bf16[2,64,2,128]{3,1,2,0:T(8,128)(2,1)S(1)}, bf16[2,64,2,128]{3,1,2,0:T(8,128)(2,1)S(1)}, u32[]{:S(2)}, u32[]{:S(2)}) %collective-permute-start) | collective-permute-done | bytes 65568 | tf_op jit(solution)/shard_map/while/body/eval_jaxpr/ppermute | solution.py:15
  36.3 5.8 %collective-permute-done = bf16[2,64,2,128]{3,1,2,0:T(8,128)(2,1)S(1)} collective-permute-done((bf16[2,64,2,128]{3,1,2,0:T(8,128)(2,1)S(1)}, bf16[2,64,2,128]{3,1,2,0:T(8,128)(2,1)S(1)}, u32[]{:S(2)}, u32[]{:S(2)}) %collective-permute-start) | collective-permute-done | bytes 65568 | tf_op jit(solution)/shard_map/while/body/eval_jaxpr/ppermute | solution.py:15
  46.2 6.1 %fusion.230 = f32[128,4096]{1,0:T(8,128)} fusion(bf16[128,1024]{1,0:T(8,128)(2,1)S(1)} %reshape.137, bf16[1024,4096]{1,0:T(8,128)(2,1)} %param.19), kind=kOutput, calls=%fused_computation.328 | convolution fusion | flops 1073741824 | bytes 10747904 | tf_op jit(solution)/shard_map/dot_general | solution.py:158
  52.7 5.1 %collective-permute-done.6 = bf16[64,1024]{1,0:T(8,128)(2,1)S(1)} collective-permute-done((bf16[64,1024]{1,0:T(8,128)(2,1)S(1)}, bf16[64,1024]{1,0:T(8,128)(2,1)S(1)}, u32[]{:S(2)}, u32[]{:S(2)}) %collective-permute-start.6) | collective-permute-done | bytes 131104 | tf_op jit(solution)/shard_map/ppermute | solution.py:25
  57.8 7.2 %collective-permute-done.7 = bf16[64,1024]{1,0:T(8,128)(2,1)S(1)} collective-permute-done((bf16[64,1024]{1,0:T(8,128)(2,1)S(1)}, bf16[64,1024]{1,0:T(8,128)(2,1)S(1)}, u32[]{:S(2)}, u32[]{:S(2)}) %collective-permute-start.7) | collective-permute-done | bytes 131104 | tf_op jit(solution)/shard_map/ppermute | solution.py:25
  65.0 17.5 %reduce-scatter.2.cloned.1.call-done = f32[128,1024]{1,0:T(8,128)} async-done(((f32[128,4096]{1,0:T(8,128)}), f32[128,1024]{1,0:T(8,128)}) %reduce-scatter.2.cloned.1.call-update) | async-done | bytes 524304 | tf_op jit(solution)/shard_map/reduce_scatter | solution.py:159
  82.5 2.2 %fusion.178 = bf16[128,1024]{1,0:T(8,128)(2,1)} fusion(f32[128,1024]{1,0:T(8,128)} %reduce-scatter.2.cloned.1.call-done, bf16[64,1024]{1,0:T(8,128)(2,1)S(1)} %collective-permute-done.7, bf16[64,1024]{1,0:T(8,128)(2,1)S(1)} %get-tuple-element.906, bf16[2,64,1024]{2,1,0:T(8,128)(2,1)S(1)} %copy-done.1, f32[16,1024]{1,0:T(8,128)S(1)} %copy-done, s32[128]{0:T(128)S(1)} %eq.30), kind=kOutput, calls=%fused_computation.245 | convolution fusion | flops 26478592 | bytes 1376768 | tf_op jit(solution)/shard_map/dot_general | solution.py:165
  84.8 16.8 %all-gather.2.cloned.1.call-done = bf16[128,4096]{1,0:T(8,128)(2,1)} async-done(((bf16[128,1024]{1,0:T(8,128)(2,1)}), bf16[128,4096]{1,0:T(8,128)(2,1)}) %all-gather.2.cloned.1.call-update) | async-done | bytes 1048592 | tf_op jit(solution)/shard_map/all_gather | solution.py:175
  101.6 6.6 %convolution_convert_fusion = bf16[128,1024]{1,0:T(8,128)(2,1)S(1)} fusion(bf16[128,4096]{1,0:T(8,128)(2,1)} %all-gather.2.cloned.1.call-done, bf16[1024,4096]{1,0:T(8,128)(2,1)} %param.19), kind=kOutput, calls=%fused_computation.222 | convolution fusion | flops 1073872896 | bytes 9699328 | tf_op jit(solution)/shard_map/dot_general | solution.py:174
  108.7 56.0 %while.57 = (s32[]{:T(128)}, f32[64,2,4,128]{3,0,2,1:T(8,128)S(1)}, f32[64,2,4,128]{3,0,2,1:T(8,128)S(1)}, bf16[2,64,2,128]{3,1,2,0:T(8,128)(2,1)S(1)}, bf16[2,6...) while((s32[]{:T(128)}, f32[64,2,4,128]{3,0,2,1:T(8,128)S(1)}, ...), condition=%wide.region_21.22_spmd.clone, body=%wide.region_20.21_spmd.clone.sunk | while | flops 169623824 | bytes 12020245 | solution.py:232
  118.8 3.7 %collective-permute-done.4 = f32[2,64,2,128]{3,1,2,0:T(8,128)S(1)} collective-permute-done((f32[2,64,2,128]{3,1,2,0:T(8,128)S(1)}, f32[2,64,2,128]{3,1,2,0:T(8,128)S(1)}, u32[]{:S(2)}, u32[]{:S(2)}) %collective-permute-start.4) | collective-permute-done | bytes 131104 | tf_op jit(solution)/shard_map/while/body/eval_jaxpr/ppermute | solution.py:15
  122.5 2.1 %collective-permute-done.5 = f32[2,64,2,128]{3,1,2,0:T(8,128)S(1)} collective-permute-done((f32[2,64,2,128]{3,1,2,0:T(8,128)S(1)}, f32[2,64,2,128]{3,1,2,0:T(8,128)S(1)}, u32[]{:S(2)}, u32[]{:S(2)}) %collective-permute-start.5) | collective-permute-done | bytes 131104 | tf_op jit(solution)/shard_map/while/body/eval_jaxpr/ppermute | solution.py:15
  130.3 3.3 %collective-permute-start.5 = (f32[2,64,2,128]{3,1,2,0:T(8,128)S(1)}, f32[2,64,2,128]{3,1,2,0:T(8,128)S(1)}, u32[]{:S(2)}, u32[]{:S(2)}) collective-permute-start(f32[2,64,2,128]{3,1,2,0:T(8,128)S(1)} %pad_maximum_fusion.7), channel_id=1, source_target_pairs={{0,4},{4,8},{8,12},{12,0},{1,5},{5,9},{9,13},{13,1},{2,6},{6,10},{... | collective-permute-start | bytes 393224 | tf_op jit(solution)/shard_map/while/body/eval_jaxpr/ppermute | solution.py:15
  143.9 2.4 %collective-permute-start.5 = (f32[2,64,2,128]{3,1,2,0:T(8,128)S(1)}, f32[2,64,2,128]{3,1,2,0:T(8,128)S(1)}, u32[]{:S(2)}, u32[]{:S(2)}) collective-permute-start(f32[2,64,2,128]{3,1,2,0:T(8,128)S(1)} %pad_maximum_fusion.7), channel_id=1, source_target_pairs={{0,4},{4,8},{8,12},{12,0},{1,5},{5,9},{9,13},{13,1},{2,6},{6,10},{... | collective-permute-start | bytes 393224 | tf_op jit(solution)/shard_map/while/body/eval_jaxpr/ppermute | solution.py:15
  147.3 2.1 %collective-permute-done.4 = f32[2,64,2,128]{3,1,2,0:T(8,128)S(1)} collective-permute-done((f32[2,64,2,128]{3,1,2,0:T(8,128)S(1)}, f32[2,64,2,128]{3,1,2,0:T(8,128)S(1)}, u32[]{:S(2)}, u32[]{:S(2)}) %collective-permute-start.4) | collective-permute-done | bytes 131104 | tf_op jit(solution)/shard_map/while/body/eval_jaxpr/ppermute | solution.py:15
  151.3 1.7 collective-permute-start.3
  157.9 2.0 %collective-permute-start.5 = (f32[2,64,2,128]{3,1,2,0:T(8,128)S(1)}, f32[2,64,2,128]{3,1,2,0:T(8,128)S(1)}, u32[]{:S(2)}, u32[]{:S(2)}) collective-permute-start(f32[2,64,2,128]{3,1,2,0:T(8,128)S(1)} %pad_maximum_fusion.7), channel_id=1, source_target_pairs={{0,4},{4,8},{8,12},{12,0},{1,5},{5,9},{9,13},{13,1},{2,6},{6,10},{... | collective-permute-start | bytes 393224 | tf_op jit(solution)/shard_map/while/body/eval_jaxpr/ppermute | solution.py:15
  160.8 2.1 %collective-permute-done.4 = f32[2,64,2,128]{3,1,2,0:T(8,128)S(1)} collective-permute-done((f32[2,64,2,128]{3,1,2,0:T(8,128)S(1)}, f32[2,64,2,128]{3,1,2,0:T(8,128)S(1)}, u32[]{:S(2)}, u32[]{:S(2)}) %collective-permute-start.4) | collective-permute-done | bytes 131104 | tf_op jit(solution)/shard_map/while/body/eval_jaxpr/ppermute | solution.py:15
  162.9 1.8 %collective-permute-done.5 = f32[2,64,2,128]{3,1,2,0:T(8,128)S(1)} collective-permute-done((f32[2,64,2,128]{3,1,2,0:T(8,128)S(1)}, f32[2,64,2,128]{3,1,2,0:T(8,128)S(1)}, u32[]{:S(2)}, u32[]{:S(2)}) %collective-permute-start.5) | collective-permute-done | bytes 131104 | tf_op jit(solution)/shard_map/while/body/eval_jaxpr/ppermute | solution.py:15
  (281 shorter events, 57.0 us)
Async XLA Ops:
  7.2 75.3 %reduce-scatter.2.cloned.1.call-start = ((), (), s32[]{:S(2)}) async-start(), calls=%async_computation.1 | async-start | bytes 2621440 | tf_op jit(solution)/shard_map/reduce_scatter | solution.py:159
  15.4 7.8 %collective-permute-start = (bf16[2,64,2,128]{3,1,2,0:T(8,128)(2,1)S(1)}, bf16[2,64,2,128]{3,1,2,0:T(8,128)(2,1)S(1)}, u32[]{:S(2)}, u32[]{:S(2)}) collective-permute-start(bf16[2,64,2,128]{3,1,2,0:T(8,128)(2,1)S(1)} %get-tuple-element.1218), channel_id=1, source_target_pairs={{0,4},{4,8},{8,12},{12,0},{1,5},{5,9},{9,13},{13,1},{2,6},{6,10},{... | collective-permute-start | bytes 196616 | tf_op jit(solution)/shard_map/while/body/eval_jaxpr/ppermute | solution.py:15
  18.5 6.1 %collective-permute-start.1 = (bf16[2,64,2,128]{3,1,2,0:T(8,128)(2,1)S(1)}, bf16[2,64,2,128]{3,1,2,0:T(8,128)(2,1)S(1)}, u32[]{:S(2)}, u32[]{:S(2)}) collective-permute-start(bf16[2,64,2,128]{3,1,2,0:T(8,128)(2,1)S(1)} %get-tuple-element.1219), channel_id=1, source_target_pairs={{0,4},{4,8},{8,12},{12,0},{1,5},{5,9},{9,13},{13,1},{2,6},{6,10},{... | collective-permute-start | bytes 196616 | tf_op jit(solution)/shard_map/while/body/eval_jaxpr/ppermute | solution.py:15
  26.5 6.1 %collective-permute-start = (bf16[2,64,2,128]{3,1,2,0:T(8,128)(2,1)S(1)}, bf16[2,64,2,128]{3,1,2,0:T(8,128)(2,1)S(1)}, u32[]{:S(2)}, u32[]{:S(2)}) collective-permute-start(bf16[2,64,2,128]{3,1,2,0:T(8,128)(2,1)S(1)} %get-tuple-element.1218), channel_id=1, source_target_pairs={{0,4},{4,8},{8,12},{12,0},{1,5},{5,9},{9,13},{13,1},{2,6},{6,10},{... | collective-permute-start | bytes 196616 | tf_op jit(solution)/shard_map/while/body/eval_jaxpr/ppermute | solution.py:15
  26.7 7.4 %collective-permute-start.1 = (bf16[2,64,2,128]{3,1,2,0:T(8,128)(2,1)S(1)}, bf16[2,64,2,128]{3,1,2,0:T(8,128)(2,1)S(1)}, u32[]{:S(2)}, u32[]{:S(2)}) collective-permute-start(bf16[2,64,2,128]{3,1,2,0:T(8,128)(2,1)S(1)} %get-tuple-element.1219), channel_id=1, source_target_pairs={{0,4},{4,8},{8,12},{12,0},{1,5},{5,9},{9,13},{13,1},{2,6},{6,10},{... | collective-permute-start | bytes 196616 | tf_op jit(solution)/shard_map/while/body/eval_jaxpr/ppermute | solution.py:15
  36.1 7.5 %collective-permute-start.1 = (bf16[2,64,2,128]{3,1,2,0:T(8,128)(2,1)S(1)}, bf16[2,64,2,128]{3,1,2,0:T(8,128)(2,1)S(1)}, u32[]{:S(2)}, u32[]{:S(2)}) collective-permute-start(bf16[2,64,2,128]{3,1,2,0:T(8,128)(2,1)S(1)} %get-tuple-element.1219), channel_id=1, source_target_pairs={{0,4},{4,8},{8,12},{12,0},{1,5},{5,9},{9,13},{13,1},{2,6},{6,10},{... | collective-permute-start | bytes 196616 | tf_op jit(solution)/shard_map/while/body/eval_jaxpr/ppermute | solution.py:15
  52.3 49.3 %all-gather.2.cloned.1.call-start = ((), (), s32[]{:S(2)}) async-start(), calls=%async_computation.2 | async-start | bytes 1310720 | tf_op jit(solution)/shard_map/all_gather | solution.py:175
  57.7 7.3 %collective-permute-start.7 = (bf16[64,1024]{1,0:T(8,128)(2,1)S(1)}, bf16[64,1024]{1,0:T(8,128)(2,1)S(1)}, u32[]{:S(2)}, u32[]{:S(2)}) collective-permute-start(bf16[64,1024]{1,0:T(8,128)(2,1)S(1)} %collective-permute-done.6), channel_id=1, source_target_pairs={{0,8},{8,0},{4,12},{12,4},{1,9},{9,1},{5,13},{13,5},{2,10},{10,2},... | collective-permute-start | bytes 393224 | tf_op jit(solution)/shard_map/ppermute | solution.py:25
  108.7 10.1 %collective-permute-start.2 = (bf16[2,64,2,128]{3,1,2,0:T(8,128)(2,1)S(1)}, bf16[2,64,2,128]{3,1,2,0:T(8,128)(2,1)S(1)}, u32[]{:S(2)}, u32[]{:S(2)}) collective-permute-start(bf16[2,64,2,128]{3,1,2,0:T(8,128)(2,1)S(1)} %copy.204), channel_id=1, source_target_pairs={{0,4},{4,8},{8,12},{12,0},{1,5},{5,9},{9,13},{13,1},{2,6},{6,10},{... | collective-permute-start | bytes 196616 | tf_op jit(solution)/shard_map/while/body/eval_jaxpr/ppermute | solution.py:15
  110.3 8.5 %collective-permute-start.3 = (bf16[2,64,2,128]{3,1,2,0:T(8,128)(2,1)S(1)}, bf16[2,64,2,128]{3,1,2,0:T(8,128)(2,1)S(1)}, u32[]{:S(2)}, u32[]{:S(2)}) collective-permute-start(bf16[2,64,2,128]{3,1,2,0:T(8,128)(2,1)S(1)} %copy.205), channel_id=1, source_target_pairs={{0,4},{4,8},{8,12},{12,0},{1,5},{5,9},{9,13},{13,1},{2,6},{6,10},{... | collective-permute-start | bytes 196616 | tf_op jit(solution)/shard_map/while/body/eval_jaxpr/ppermute | solution.py:15
  114.8 7.6 %collective-permute-start.4 = (f32[2,64,2,128]{3,1,2,0:T(8,128)S(1)}, f32[2,64,2,128]{3,1,2,0:T(8,128)S(1)}, u32[]{:S(2)}, u32[]{:S(2)}) collective-permute-start(f32[2,64,2,128]{3,1,2,0:T(8,128)S(1)} %pad_maximum_fusion.6), channel_id=1, source_target_pairs={{0,4},{4,8},{8,12},{12,0},{1,5},{5,9},{9,13},{13,1},{2,6},{6,10},{... | collective-permute-start | bytes 393224 | tf_op jit(solution)/shard_map/while/body/eval_jaxpr/ppermute | solution.py:15
  117.3 7.3 %collective-permute-start.5 = (f32[2,64,2,128]{3,1,2,0:T(8,128)S(1)}, f32[2,64,2,128]{3,1,2,0:T(8,128)S(1)}, u32[]{:S(2)}, u32[]{:S(2)}) collective-permute-start(f32[2,64,2,128]{3,1,2,0:T(8,128)S(1)} %pad_maximum_fusion.7), channel_id=1, source_target_pairs={{0,4},{4,8},{8,12},{12,0},{1,5},{5,9},{9,13},{13,1},{2,6},{6,10},{... | collective-permute-start | bytes 393224 | tf_op jit(solution)/shard_map/while/body/eval_jaxpr/ppermute | solution.py:15
  124.6 10.0 %collective-permute-start.2 = (bf16[2,64,2,128]{3,1,2,0:T(8,128)(2,1)S(1)}, bf16[2,64,2,128]{3,1,2,0:T(8,128)(2,1)S(1)}, u32[]{:S(2)}, u32[]{:S(2)}) collective-permute-start(bf16[2,64,2,128]{3,1,2,0:T(8,128)(2,1)S(1)} %copy.204), channel_id=1, source_target_pairs={{0,4},{4,8},{8,12},{12,0},{1,5},{5,9},{9,13},{13,1},{2,6},{6,10},{... | collective-permute-start | bytes 196616 | tf_op jit(solution)/shard_map/while/body/eval_jaxpr/ppermute | solution.py:15
  124.6 10.0 %collective-permute-start.3 = (bf16[2,64,2,128]{3,1,2,0:T(8,128)(2,1)S(1)}, bf16[2,64,2,128]{3,1,2,0:T(8,128)(2,1)S(1)}, u32[]{:S(2)}, u32[]{:S(2)}) collective-permute-start(bf16[2,64,2,128]{3,1,2,0:T(8,128)(2,1)S(1)} %copy.205), channel_id=1, source_target_pairs={{0,4},{4,8},{8,12},{12,0},{1,5},{5,9},{9,13},{13,1},{2,6},{6,10},{... | collective-permute-start | bytes 196616 | tf_op jit(solution)/shard_map/while/body/eval_jaxpr/ppermute | solution.py:15
  127.9 8.0 %collective-permute-start.4 = (f32[2,64,2,128]{3,1,2,0:T(8,128)S(1)}, f32[2,64,2,128]{3,1,2,0:T(8,128)S(1)}, u32[]{:S(2)}, u32[]{:S(2)}) collective-permute-start(f32[2,64,2,128]{3,1,2,0:T(8,128)S(1)} %pad_maximum_fusion.6), channel_id=1, source_target_pairs={{0,4},{4,8},{8,12},{12,0},{1,5},{5,9},{9,13},{13,1},{2,6},{6,10},{... | collective-permute-start | bytes 393224 | tf_op jit(solution)/shard_map/while/body/eval_jaxpr/ppermute | solution.py:15
  130.3 7.0 %collective-permute-start.5 = (f32[2,64,2,128]{3,1,2,0:T(8,128)S(1)}, f32[2,64,2,128]{3,1,2,0:T(8,128)S(1)}, u32[]{:S(2)}, u32[]{:S(2)}) collective-permute-start(f32[2,64,2,128]{3,1,2,0:T(8,128)S(1)} %pad_maximum_fusion.7), channel_id=1, source_target_pairs={{0,4},{4,8},{8,12},{12,0},{1,5},{5,9},{9,13},{13,1},{2,6},{6,10},{... | collective-permute-start | bytes 393224 | tf_op jit(solution)/shard_map/while/body/eval_jaxpr/ppermute | solution.py:15
  137.2 10.0 %collective-permute-start.2 = (bf16[2,64,2,128]{3,1,2,0:T(8,128)(2,1)S(1)}, bf16[2,64,2,128]{3,1,2,0:T(8,128)(2,1)S(1)}, u32[]{:S(2)}, u32[]{:S(2)}) collective-permute-start(bf16[2,64,2,128]{3,1,2,0:T(8,128)(2,1)S(1)} %copy.204), channel_id=1, source_target_pairs={{0,4},{4,8},{8,12},{12,0},{1,5},{5,9},{9,13},{13,1},{2,6},{6,10},{... | collective-permute-start | bytes 196616 | tf_op jit(solution)/shard_map/while/body/eval_jaxpr/ppermute | solution.py:15
  138.6 8.7 %collective-permute-start.3 = (bf16[2,64,2,128]{3,1,2,0:T(8,128)(2,1)S(1)}, bf16[2,64,2,128]{3,1,2,0:T(8,128)(2,1)S(1)}, u32[]{:S(2)}, u32[]{:S(2)}) collective-permute-start(bf16[2,64,2,128]{3,1,2,0:T(8,128)(2,1)S(1)} %copy.205), channel_id=1, source_target_pairs={{0,4},{4,8},{8,12},{12,0},{1,5},{5,9},{9,13},{13,1},{2,6},{6,10},{... | collective-permute-start | bytes 196616 | tf_op jit(solution)/shard_map/while/body/eval_jaxpr/ppermute | solution.py:15
  142.6 6.8 %collective-permute-start.4 = (f32[2,64,2,128]{3,1,2,0:T(8,128)S(1)}, f32[2,64,2,128]{3,1,2,0:T(8,128)S(1)}, u32[]{:S(2)}, u32[]{:S(2)}) collective-permute-start(f32[2,64,2,128]{3,1,2,0:T(8,128)S(1)} %pad_maximum_fusion.6), channel_id=1, source_target_pairs={{0,4},{4,8},{8,12},{12,0},{1,5},{5,9},{9,13},{13,1},{2,6},{6,10},{... | collective-permute-start | bytes 393224 | tf_op jit(solution)/shard_map/while/body/eval_jaxpr/ppermute | solution.py:15
  143.9 6.9 %collective-permute-start.5 = (f32[2,64,2,128]{3,1,2,0:T(8,128)S(1)}, f32[2,64,2,128]{3,1,2,0:T(8,128)S(1)}, u32[]{:S(2)}, u32[]{:S(2)}) collective-permute-start(f32[2,64,2,128]{3,1,2,0:T(8,128)S(1)} %pad_maximum_fusion.7), channel_id=1, source_target_pairs={{0,4},{4,8},{8,12},{12,0},{1,5},{5,9},{9,13},{13,1},{2,6},{6,10},{... | collective-permute-start | bytes 393224 | tf_op jit(solution)/shard_map/while/body/eval_jaxpr/ppermute | solution.py:15
  150.8 10.0 %collective-permute-start.2 = (bf16[2,64,2,128]{3,1,2,0:T(8,128)(2,1)S(1)}, bf16[2,64,2,128]{3,1,2,0:T(8,128)(2,1)S(1)}, u32[]{:S(2)}, u32[]{:S(2)}) collective-permute-start(bf16[2,64,2,128]{3,1,2,0:T(8,128)(2,1)S(1)} %copy.204), channel_id=1, source_target_pairs={{0,4},{4,8},{8,12},{12,0},{1,5},{5,9},{9,13},{13,1},{2,6},{6,10},{... | collective-permute-start | bytes 196616 | tf_op jit(solution)/shard_map/while/body/eval_jaxpr/ppermute | solution.py:15
  151.3 9.5 %collective-permute-start.3 = (bf16[2,64,2,128]{3,1,2,0:T(8,128)(2,1)S(1)}, bf16[2,64,2,128]{3,1,2,0:T(8,128)(2,1)S(1)}, u32[]{:S(2)}, u32[]{:S(2)}) collective-permute-start(bf16[2,64,2,128]{3,1,2,0:T(8,128)(2,1)S(1)} %copy.205), channel_id=1, source_target_pairs={{0,4},{4,8},{8,12},{12,0},{1,5},{5,9},{9,13},{13,1},{2,6},{6,10},{... | collective-permute-start | bytes 196616 | tf_op jit(solution)/shard_map/while/body/eval_jaxpr/ppermute | solution.py:15
  156.0 6.8 %collective-permute-start.4 = (f32[2,64,2,128]{3,1,2,0:T(8,128)S(1)}, f32[2,64,2,128]{3,1,2,0:T(8,128)S(1)}, u32[]{:S(2)}, u32[]{:S(2)}) collective-permute-start(f32[2,64,2,128]{3,1,2,0:T(8,128)S(1)} %pad_maximum_fusion.6), channel_id=1, source_target_pairs={{0,4},{4,8},{8,12},{12,0},{1,5},{5,9},{9,13},{13,1},{2,6},{6,10},{... | collective-permute-start | bytes 393224 | tf_op jit(solution)/shard_map/while/body/eval_jaxpr/ppermute | solution.py:15
  157.9 6.8 %collective-permute-start.5 = (f32[2,64,2,128]{3,1,2,0:T(8,128)S(1)}, f32[2,64,2,128]{3,1,2,0:T(8,128)S(1)}, u32[]{:S(2)}, u32[]{:S(2)}) collective-permute-start(f32[2,64,2,128]{3,1,2,0:T(8,128)S(1)} %pad_maximum_fusion.7), channel_id=1, source_target_pairs={{0,4},{4,8},{8,12},{12,0},{1,5},{5,9},{9,13},{13,1},{2,6},{6,10},{... | collective-permute-start | bytes 393224 | tf_op jit(solution)/shard_map/while/body/eval_jaxpr/ppermute | solution.py:15
  (6 other events, 140.7 us)
Sparse Core Ops, SparseCore 0:
  52.4 29.9 reduce-scatter.1
  84.8 16.6 all-gather.1
where the time goes:
time: 175 us; the launch traced here: 174 us
  waiting for transfers between devices  75.5 us (43%)
  matrix products  45.2 us (26%)
  starting transfers between devices  27.1 us (15%)
  between operations  14.4 us (8%)
  local copies, waits for them, and re-layouts  7.56 us (4%)
  other arithmetic  3.55 us (2%)
    ppermute x22, waiting for transfers between devices, passed_along(): return lax.ppermute(value, axis, pairs)  28.9 us
    ppermute x22, starting transfers between devices, passed_along(): return lax.ppermute(value, axis, pairs)  26.8 us
    reduce_scatter x1, waiting for transfers between devices, on_device(): lax.psum_scatter(partial_proj, 'head', scatter_dimension=1, tiled=True)  17.5 us
    all_gather x1, waiting for transfers between devices, on_device(): lax.all_gather(grad_proj, 'head', axis=1, tiled=True)  16.8 us
    ppermute x2, waiting for transfers between devices, partner(): return lax.ppermute(block, axis, route)  12.2 us
    dot_general x16, matrix products, attend(): jnp.einsum('kgrp,pkd->kgrd', weights, value_rows.astype(jnp.float32), pre...  7.16 us
    dot_general x1, matrix products, on_device(): lax.dot_general(lax.all_gather(grad_proj, 'head', axis=1, tiled=True), ou...  6.62 us
    dot_general x1, matrix products, on_device(): jnp.dot(flat_attn, out_weight, preferred_element_type=jnp.float32)  6.05 us
  transfers between devices with their start and end apart: 26, of which 15 were waited for; matrix products, arithmetic and copies ran while one was open for 14% of the time, Pallas kernels for 0%

commit v1 on v0

v1 whole, which is shorter than its diff:
```python
import functools

import jax
import jax.numpy as jnp
from jax import lax
from jax.experimental import pallas as pl
from jax.experimental.pallas import tpu as pltpu
from jax.sharding import PartitionSpec as P

HEAD_DIM = 128
BIG_NEG = -1e30
LOG2E = 1.4426950408889634
F32 = jnp.float32
BF16 = jnp.bfloat16
VMEM = pl.BlockSpec(memory_space=pltpu.VMEM)
ANY = pl.BlockSpec(memory_space=pl.ANY)


def across(block, axis, bit):
    count = lax.axis_size(axis)
    return lax.ppermute(block, axis, [(i, i ^ bit) for i in range(count)])


def bits_of(count):
    return [1 << b for b in range(count.bit_length() - 1)]


def gather_blocks(own, axis):
    blocks = {0: own}
    for bit in reversed(bits_of(lax.axis_size(axis))):
        for s in sorted(blocks):
            blocks[s ^ bit] = across(blocks[s], axis, bit)
    return [blocks[s] for s in range(len(blocks))]


def nt(a, b):
    return lax.dot_general(a, b, (((1,), (1,)), ((), ())), preferred_element_type=F32)


def nn(a, b):
    return jnp.dot(a, b, preferred_element_type=F32)


def call(body, out, args, specs, mib, name, cost=None):
    return pl.pallas_call(
        body,
        out_shape=out,
        in_specs=specs,
        out_specs=jax.tree.map(lambda _: VMEM, out),
        compiler_params=pltpu.CompilerParams(vmem_limit_bytes=mib << 20),
        cost_estimate=cost,
        name=name,
    )(*args)


def cost(flops, moved):
    return pl.CostEstimate(flops=flops, bytes_accessed=moved, transcendentals=0)


def stacked_heads(ref, span, rows, group, per_group):
    pieces = [
        ref[span * rows : (span + 1) * rows, h * HEAD_DIM : (h + 1) * HEAD_DIM]
        for h in range(group * per_group, (group + 1) * per_group)
    ]
    return jnp.concatenate(pieces, axis=0)


def stacked_keys(refs, part, rows, group):
    cols = slice(group * HEAD_DIM, (group + 1) * HEAD_DIM)
    return jnp.concatenate([r[part * rows : (part + 1) * rows, cols] for r in refs], axis=0)


def diagonal_mask(owner_xor, device, rows, columns, upper):
    owner = device ^ owner_xor
    key = lax.broadcasted_iota(jnp.int32, (rows, columns), 0)
    query = lax.broadcasted_iota(jnp.int32, (rows, columns), 1) & (rows - 1)
    ahead = (device - owner if upper else owner - device) * rows
    return key + ahead <= query


def attention_kernel(n, rows, kv_local, per_group, q_ref, *refs):
    kv_refs, (att_ref, low_ref, high_ref) = refs[:n], refs[n:]
    device = lax.axis_index("ctx")
    columns = per_group * rows
    scale = HEAD_DIM**-0.5 * LOG2E
    masks = {
        (s, upper): diagonal_mask(s, device, rows, columns, upper)
        for s in range(n)
        for upper in (False, True)
    }
    for group in range(kv_local):
        keys = [stacked_keys(kv_refs, part, rows, group) for part in (0, 1)]
        vals = [stacked_keys(kv_refs, part, rows, group) for part in (2, 3)]
        vals_t = [v.astype(F32).T.astype(BF16) for v in vals]
        for span in (0, 1):
            query = stacked_heads(q_ref, span, rows, group, per_group)
            tiles = []
            for half in range(span + 1):
                tile = nt(keys[half], query) * scale
                if half == span:
                    tile = jnp.concatenate(
                        [
                            jnp.where(
                                masks[s, span == 1], tile[s * rows : (s + 1) * rows], BIG_NEG
                            )
                            for s in range(n)
                        ],
                        axis=0,
                    )
                tiles.append(tile)
            top = functools.reduce(
                jnp.maximum, [jnp.max(t, axis=0, keepdims=True) for t in tiles]
            )
            tiles = [jnp.exp2(t - top) for t in tiles]
            total = sum(jnp.sum(t, axis=0, keepdims=True) for t in tiles)
            inverse = 1.0 / total
            mixed = jnp.zeros((HEAD_DIM, columns), F32)
            for half, tile in enumerate(tiles):
                probs = tile * inverse
                if span == 0:
                    low_ref[group] = probs
                else:
                    high_ref[group, half * n * rows : (half + 1) * n * rows] = probs
                mixed += nn(vals_t[half], probs.astype(BF16))
            out = mixed.T.astype(BF16)
            for i in range(per_group):
                h = group * per_group + i
                att_ref[
                    span * rows : (span + 1) * rows, h * HEAD_DIM : (h + 1) * HEAD_DIM
                ] = out[i * rows : (i + 1) * rows]


def project_kernel(width, offsets, a_ref, w_ref, *outs):
    head = lax.axis_index("head")
    for s, out in zip(offsets, outs):
        start = pl.multiple_of((head ^ s) * width, width)
        out[...] = nn(a_ref[...], w_ref[:, pl.ds(start, width)]).astype(out.dtype)


def hold_kernel(w_ref, o_ref, sem):
    copy = pltpu.make_async_copy(w_ref, o_ref, sem)
    copy.start()
    copy.wait()


def prepare_kernel(lang_ref, table_ref, residual_ref, low_ref, high_ref, scale_ref, gap_ref):
    rows = low_ref.shape[0]
    kinds = table_ref.shape[0]
    chosen = lang_ref[...] == lax.broadcasted_iota(jnp.int32, (2 * rows, kinds), 1)
    scale_ref[...] = jnp.dot(
        chosen.astype(F32),
        table_ref[...],
        precision=lax.Precision.HIGHEST,
        preferred_element_type=F32,
    )
    for span, target in ((0, low_ref), (1, high_ref)):
        part = slice(span * rows, (span + 1) * rows)
        gap_ref[part] = residual_ref[part].astype(F32) - target[...].astype(F32)


def backward_kernel(n, nh, rows, kv_local, per_group, width, q_ref, low_ref, high_ref, w_ref, *refs):
    kv_refs, g_refs, outs = refs[:n], refs[n : n + nh], refs[n + nh :]
    dq_ref, dkv_refs = outs[0], outs[1:]
    head = lax.axis_index("head")
    columns = per_group * rows
    scale = HEAD_DIM**-0.5
    grad = None
    for s in range(nh):
        start = pl.multiple_of((head ^ s) * width, width)
        part = nt(g_refs[s][...], w_ref[:, pl.ds(start, width)])
        grad = part if grad is None else grad + part
    grad = grad.astype(BF16)
    for group in range(kv_local):
        keys = [stacked_keys(kv_refs, part, rows, group) for part in (0, 1)]
        vals = [stacked_keys(kv_refs, part, rows, group) for part in (2, 3)]
        keys_t = [k.astype(F32).T.astype(BF16) for k in keys]
        grad_k, grad_v = [None, None], [None, None]
        for span in (0, 1):
            query = stacked_heads(q_ref, span, rows, group, per_group)
            out = stacked_heads(grad, span, rows, group, per_group)
            probs = (
                [low_ref[group]]
                if span == 0
                else [high_ref[group, h * n * rows : (h + 1) * n * rows] for h in (0, 1)]
            )
            terms = [p * nt(vals[half], out) for half, p in enumerate(probs)]
            delta = sum(jnp.sum(t, axis=0, keepdims=True) for t in terms)
            grad_q = jnp.zeros((HEAD_DIM, columns), F32)
            for half, (prob, term) in enumerate(zip(probs, terms)):
                step = (term - prob * delta).astype(BF16)
                grad_q += nn(keys_t[half], step)
                dv, dk = nn(prob.astype(BF16), out), nn(step, query)
                grad_v[half] = dv if grad_v[half] is None else grad_v[half] + dv
                grad_k[half] = dk if grad_k[half] is None else grad_k[half] + dk
            grad_q = (grad_q * scale).T
            for i in range(per_group):
                h = group * per_group + i
                dq_ref[span * rows : (span + 1) * rows, h * HEAD_DIM : (h + 1) * HEAD_DIM] = (
                    grad_q[i * rows : (i + 1) * rows]
                )
        cols = slice(group * HEAD_DIM, (group + 1) * HEAD_DIM)
        for half in (0, 1):
            for s, ref in enumerate(dkv_refs):
                block = slice(s * rows, (s + 1) * rows)
                ref[half * rows : (half + 1) * rows, cols] = (grad_k[half][block] * scale).astype(
                    ref.dtype
                )
                ref[(2 + half) * rows : (3 + half) * rows, cols] = grad_v[half][block].astype(
                    ref.dtype
                )


def reduce_blocks(blocks, axis):
    blocks = dict(enumerate(blocks))
    for bit in bits_of(lax.axis_size(axis)):
        for s in sorted((s for s in blocks if s & bit), reverse=True):
            got = across(blocks.pop(s).astype(BF16), axis, bit)
            blocks[s ^ bit] = blocks[s ^ bit].astype(F32) + got.astype(F32)
    return blocks[0]


def on_device(queries, keys, values, residual, targets, lang_ids, lang_scale, out_weight):
    n, nh = lax.axis_size("ctx"), lax.axis_size("head")
    rows = queries.shape[1]
    kv_width, q_width = keys.shape[2], queries.shape[2]
    kv_local, q_local = kv_width // HEAD_DIM, q_width // HEAD_DIM
    per_group = q_local // kv_local
    width = residual.shape[2]
    columns = per_group * rows

    kv_own = jnp.concatenate([keys, values]).reshape(4 * rows, kv_width)
    kv = gather_blocks(kv_own, "ctx")
    upper_targets = across(targets[1], "ctx", n - 1)
    weight = pl.pallas_call(
        hold_kernel,
        out_shape=pltpu.VMEM(out_weight.shape, BF16),
        in_specs=[pl.BlockSpec(memory_space=pltpu.HBM)],
        out_specs=VMEM,
        scratch_shapes=[pltpu.SemaphoreType.DMA],
        compiler_params=pltpu.CompilerParams(vmem_limit_bytes=1 << 20),
        name="hold",
    )(out_weight)
    flat_q = queries.reshape(2 * rows, q_width)
    attended, low_probs, high_probs = call(
        functools.partial(attention_kernel, n, rows, kv_local, per_group),
        (
            pltpu.VMEM((2 * rows, q_width), BF16),
            pltpu.VMEM((kv_local, n * rows, columns), F32),
            pltpu.VMEM((kv_local, 2 * n * rows, columns), F32),
        ),
        (flat_q, *kv),
        [VMEM] * (1 + n),
        16,
        "attention",
        cost(12 * n * rows * columns * HEAD_DIM * kv_local, 1 << 21),
    )
    row_scales, gap = call(
        prepare_kernel,
        (pltpu.VMEM((2 * rows, width), F32), pltpu.VMEM((2 * rows, width), F32)),
        (
            lang_ids.reshape(2 * rows, 1),
            lang_scale,
            residual.reshape(2 * rows, width),
            targets[0],
            upper_targets,
        ),
        [VMEM] * 5,
        16,
        "prepare",
    )
    order = sorted(range(nh), key=lambda s: (s & 1 == 0, -s))
    parts = {}
    for offsets in (order[: nh // 4], order[nh // 4 :]):
        got = call(
            functools.partial(project_kernel, width, offsets),
            tuple(pltpu.VMEM((2 * rows, width), BF16 if s & 1 else F32) for s in offsets),
            (attended, weight),
            [VMEM] * 2,
            16,
            "project",
            cost(4 * rows * q_width * width * len(offsets), q_width * width * 2 * len(offsets)),
        )
        parts.update(zip(offsets, got))
    projected = reduce_blocks([parts[s] for s in range(nh)], "head")
    grad_proj = ((gap + projected * row_scales) * row_scales).astype(BF16)
    grads = gather_blocks(grad_proj, "head")
    outs = call(
        functools.partial(backward_kernel, n, nh, rows, kv_local, per_group, width),
        (
            jax.ShapeDtypeStruct((2 * rows, q_width), F32),
            pltpu.VMEM((4 * rows, kv_width), F32),
            *(pltpu.VMEM((4 * rows, kv_width), BF16) for _ in range(n - 1)),
        ),
        (flat_q, low_probs, high_probs, weight, *kv, *grads),
        [VMEM] * (4 + n + nh),
        20,
        "backward",
        cost(1 << 31, 1 << 24),
    )
    grad_kv = reduce_blocks(outs[1:], "ctx")
    return (
        outs[0].reshape(2, rows, q_width),
        grad_kv[: 2 * rows].reshape(2, rows, kv_width),
        grad_kv[2 * rows :].reshape(2, rows, kv_width),
    )


def solution(mesh):
    split = P(None, ("groups", "ctx"), "head")
    in_specs = (
        split,
        split,
        split,
        split,
        split,
        P(None, ("groups", "ctx")),
        P(None, "head"),
        P("head", None),
    )
    return jax.shard_map(
        on_device, mesh=mesh, in_specs=in_specs, out_specs=(split, split, split), check_vma=False
    )
```

time: 175 us -> 67.1 us (0.38)
  waiting for transfers between devices: 75.5 us -> 26.7 us
  matrix products: 45.2 us -> 0 us
  between operations: 14.4 us -> 0.78 us
  Pallas kernels: 0 us -> 9.36 us
  starting transfers between devices: 27.1 us -> 18.7 us
    dot_general x115 -> x0, matrix products: 45.2 us -> none  [the longest x16 7.16 us: attend(): jnp.einsum('kgrp,pkd->kgrd', weights, value_rows.astype(jnp.float32), pre...]
    reduce_scatter x1 -> x0, waiting for transfers between devices: 17.5 us -> none  [on_device(): lax.psum_scatter(partial_proj, 'head', scatter_dimension=1, tiled=True)]
    all_gather x1 -> x0, waiting for transfers between devices: 16.8 us -> none  [on_device(): lax.all_gather(grad_proj, 'head', axis=1, tiled=True)]
    ppermute x24 -> x13, waiting for transfers between devices: 41.1 us -> 26.7 us  [across(): return lax.ppermute(block, axis, [(i, i ^ bit) for i in range(count)])]
    pallas_call x0 -> x6, Pallas kernels: none -> 9.36 us  [the longest x5 8.79 us: call(): pl.pallas_call(body, out_shape=out, in_specs=specs, out_specs=jax.tree.ma...]
    ppermute x24 -> x13, starting transfers between devices: 26.9 us -> 18.7 us  [across(): return lax.ppermute(block, axis, [(i, i ^ bit) for i in range(count)])]
    unnamed x13 -> x16, local copies, waits for them, and re-layouts: 1.02 us -> 6.8 us
    reshape x5 -> x1, local copies, waits for them, and re-layouts: 2.79 us -> 0.13 us  [on_device(): lang_ids.reshape(2 * rows, 1)]
  transfers between devices with their start and end apart: 26 -> 13, of which waited for: 15 -> 7; matrix products, arithmetic and copies ran while one was open for 14% -> 2% of each run, Pallas kernels for 0% -> 4%
where the time goes in v1:
time: 67.1 us; the launch traced here: 66.8 us
  waiting for transfers between devices  26.7 us (40%)
  starting transfers between devices  18.7 us (28%)
  Pallas kernels  9.36 us (14%)
  local copies, waits for them, and re-layouts  8.32 us (12%)
  other arithmetic  2.98 us (4%)
  between operations  0.78 us (1%)
    ppermute x13, waiting for transfers between devices, across(): return lax.ppermute(block, axis, [(i, i ^ bit) for i in range(count)])  26.7 us
    ppermute x13, starting transfers between devices, across(): return lax.ppermute(block, axis, [(i, i ^ bit) for i in range(count)])  18.7 us
    pallas_call x5, Pallas kernels, call(): pl.pallas_call(body, out_shape=out, in_specs=specs, out_specs=jax.tree.ma...  8.79 us
    unnamed x16, local copies, waits for them, and re-layouts  6.8 us
  transfers between devices with their start and end apart: 13, of which 7 were waited for; matrix products, arithmetic and copies ran while one was open for 2% of the time, Pallas kernels for 4%

profile of v1, /device:TPU:0, one launch (start us, length us, event | category | flops | bytes accessed | tf_op | source)
XLA Modules:
  0.0 66.8 jit_solution(11986262559858948306)
XLA Ops:
  0.6 0.9 %pad_maximum_fusion = bf16[4,64,256]{2,1,0:T(8,128)(2,1)S(1)} fusion(bf16[2,64,256]{2,1,0:T(8,128)(2,1)} %param.10, bf16[2,64,256]{2,1,0:T(8,128)(2,1)} %param.9), kind=kLoop, calls=%fused_computation.4 | loop fusion | flops 65536 | bytes 262144 | tf_op jit(solution)/shard_map/concatenate | solution.py:231
  1.6 4.1 %collective-permute-start.1 = (bf16[256,256]{1,0:T(8,128)(2,1)S(1)}, bf16[256,256]{1,0:T(8,128)(2,1)S(1)}, u32[]{:S(2)}, u32[]{:S(2)}) collective-permute-start(bf16[256,256]{1,0:T(8,128)(2,1)S(1)} %bitcast.10), channel_id=1, source_target_pairs={{0,8},{4,12},{8,0},{12,4},{1,9},{5,13},{9,1},{13,5},{2,10},{6,14},... | collective-permute-start | bytes 393224 | tf_op jit(solution)/shard_map/ppermute | solution.py:21
  5.7 1.6 %collective-permute-start = (bf16[256,256]{1,0:T(8,128)(2,1)S(1)}, bf16[256,256]{1,0:T(8,128)(2,1)S(1)}, u32[]{:S(2)}, u32[]{:S(2)}) collective-permute-start(bf16[256,256]{1,0:T(8,128)(2,1)S(1)} %bitcast.11), channel_id=1, source_target_pairs={{0,4},{4,0},{8,12},{12,8},{1,5},{5,1},{9,13},{13,9},{2,6},{6,2},{1... | collective-permute-start | bytes 393224 | tf_op jit(solution)/shard_map/ppermute | solution.py:21
  7.2 4.8 %collective-permute-done.1.refs_2_ = bf16[256,256]{1,0:T(8,128)(2,1)S(1)} collective-permute-done((bf16[256,256]{1,0:T(8,128)(2,1)S(1)}, bf16[256,256]{1,0:T(8,128)(2,1)S(1)}, u32[]{:S(2)}, u32[]{:S(2)}) %collective-permute-start.1) | collective-permute-done | bytes 131104 | tf_op jit(solution)/shard_map/ppermute | solution.py:21
  12.1 0.6 collective-permute-start.2
  12.7 3.4 %copy-done.2 = bf16[1024,4096]{1,0:T(8,128)(2,1)S(1)} copy-done((bf16[1024,4096]{1,0:T(8,128)(2,1)S(1)}, bf16[1024,4096]{1,0:T(8,128)(2,1)}, u32[]{:S(2)}) %copy-start.2) | copy-done | bytes 8388632
  17.1 1.4 %attention.1 = (bf16[128,1024]{1,0:T(8,128)(2,1)S(1)}, f32[2,256,256]{2,1,0:T(8,128)S(1)}, f32[2,512,256]{2,1,0:T(8,128)S(1)}) custom-call(bf16[128,1024]{1,0:T(8,128)(2,1)S(1)} %bitcast.14, bf16[256,256]{1,0:T(8,128)(2,1)S(1)} %bitcast.12, bf16[256,256]{1,0:T(8,128)(2,1)S(1)} %collective-permute-done.refs_1_, ...), custom_call_target="tpu_custom_call" | custom-call | flops 201326592 | bytes 2097152 | tf_op jit(solution)/shard_map/attention/pallas_call | solution.py:45
  19.1 1.2 %project.2 = (bf16[128,1024]{1,0:T(8,128)(2,1)}, f32[128,1024]{1,0:T(8,128)S(1)}, f32[128,1024]{1,0:T(8,128)S(1)}) custom-call(bf16[128,1024]{1,0:T(8,128)(2,1)S(1)} %get-tuple-element.19.a_ref, bf16[1024,4096]{1,0:T(8,128)(2,1)S(1)} %hold.1.w_ref), custom_call_target="tpu_custom_call" | custom-call | flops 805306368 | bytes 6291456 | tf_op jit(solution)/shard_map/project/pallas_call | solution.py:45
  20.8 0.8 %add_convert_fusion = bf16[128,1024]{1,0:T(8,128)(2,1)} fusion(f32[128,1024]{1,0:T(8,128)S(1)} %get-tuple-element.22, bf16[128,1024]{1,0:T(8,128)(2,1)S(1)} %collective-permute-done.5), kind=kLoop, calls=%fused_computation.1 | loop fusion | flops 393216 | bytes 1048576 | tf_op jit(solution)/shard_map/convert_element_type | solution.py:217
  21.5 1.5 %collective-permute-start.6 = (bf16[128,1024]{1,0:T(8,128)(2,1)}, bf16[128,1024]{1,0:T(8,128)(2,1)}, u32[]{:S(2)}, u32[]{:S(2)}) collective-permute-start(bf16[128,1024]{1,0:T(8,128)(2,1)} %add_convert_fusion), channel_id=1, source_target_pairs={{0,2},{1,3},{2,0},{3,1},{4,6},{5,7},{6,4},{7,5},{8,10},{9,11},{10,... | collective-permute-start | bytes 786440 | tf_op jit(solution)/shard_map/ppermute | solution.py:21
  23.1 0.7 %slice_bitcast_fusion = (bf16[64,1024]{1,0:T(8,128)(2,1)}, bf16[64,1024]{1,0:T(8,128)(2,1)S(1)}) fusion(bf16[2,64,1024]{2,1,0:T(8,128)(2,1)S(1)} %copy-done.6), kind=kLoop, calls=%fused_computation.5 | loop fusion | bytes 524288 | tf_op jit(solution)/shard_map/squeeze | solution.py:233
  23.8 3.8 %collective-permute-start.3 = (bf16[64,1024]{1,0:T(8,128)(2,1)}, bf16[64,1024]{1,0:T(8,128)(2,1)S(1)}, u32[]{:S(2)}, u32[]{:S(2)}) collective-permute-start(bf16[64,1024]{1,0:T(8,128)(2,1)} %get-tuple-element.31), channel_id=1, source_target_pairs={{0,12},{4,8},{8,4},{12,0},{1,13},{5,9},{9,5},{13,1},{2,14},{6,10},... | collective-permute-start | bytes 393224 | tf_op jit(solution)/shard_map/ppermute | solution.py:21
  27.7 3.6 %collective-permute-done.3.high_ref = bf16[64,1024]{1,0:T(8,128)(2,1)S(1)} collective-permute-done((bf16[64,1024]{1,0:T(8,128)(2,1)}, bf16[64,1024]{1,0:T(8,128)(2,1)S(1)}, u32[]{:S(2)}, u32[]{:S(2)}) %collective-permute-start.3) | collective-permute-done | bytes 131104 | tf_op jit(solution)/shard_map/ppermute | solution.py:21
  31.3 0.6 prepare.1
  32.0 1.2 %multiply_convert_fusion.refs_4_ = bf16[128,1024]{1,0:T(8,128)(2,1)S(1)} fusion(f32[128,1024]{1,0:T(8,128)S(1)} %get-tuple-element.23, f32[128,1024]{1,0:T(8,128)S(1)} %get-tuple-element.18, bf16[128,1024]{1,0:T(8,128)(2,1)} %collective-permute-done.6, f32[128,1024]{1,0:T(8,128)S(1)} %get-tuple-element.20, bf16[128,1024]{1,0:T(8,128)(2,1)} %collective-permute-done.4), kind=kLoop, calls=%fused_computation | loop fusion | flops 1048576 | bytes 2359296 | tf_op jit(solution)/shard_map/convert_element_type | solution.py:285
  33.8 6.8 %collective-permute-done.8.refs_6_ = bf16[128,1024]{1,0:T(8,128)(2,1)S(1)} collective-permute-done((bf16[128,1024]{1,0:T(8,128)(2,1)S(1)}, bf16[128,1024]{1,0:T(8,128)(2,1)S(1)}, u32[]{:S(2)}, u32[]{:S(2)}) %collective-permute-start.8) | collective-permute-done | bytes 262176 | tf_op jit(solution)/shard_map/ppermute | solution.py:21
  40.5 1.5 %collective-permute-done.9.refs_7_ = bf16[128,1024]{1,0:T(8,128)(2,1)S(1)} collective-permute-done((bf16[128,1024]{1,0:T(8,128)(2,1)S(1)}, bf16[128,1024]{1,0:T(8,128)(2,1)S(1)}, u32[]{:S(2)}, u32[]{:S(2)}) %collective-permute-start.9) | collective-permute-done | bytes 262176 | tf_op jit(solution)/shard_map/ppermute | solution.py:21
  42.1 3.4 %copy-done.1 = bf16[1024,4096]{1,0:T(8,128)(2,1)S(1)} copy-done((bf16[1024,4096]{1,0:T(8,128)(2,1)S(1)}, bf16[1024,4096]{1,0:T(8,128)(2,1)}, u32[]{:S(2)}) %copy-start.1) | copy-done | bytes 8388632
  45.5 5.1 %backward.1 = (f32[128,1024]{1,0:T(8,128)}, f32[256,256]{1,0:T(8,128)S(1)}, bf16[256,256]{1,0:T(8,128)(2,1)S(1)}, bf16[256,256]{1,0:T(8,128)(2,1)S(1)}, bf16[256,256]{1,0:T(8,128)(2,1)S(1)}) custom-call(bf16[128,1024]{1,0:T(8,128)(2,1)S(1)} %bitcast.15, f32[2,256,256]{2,1,0:T(8,128)S(1)} %get-tuple-element.16.low_ref, ...), custom_call_target="tpu_custom_call" | custom-call | flops 2147483648 | bytes 16777216 | tf_op jit(solution)/shard_map/backward/pallas_call | solution.py:45
  50.5 2.9 %collective-permute-start.11 = (bf16[256,256]{1,0:T(8,128)(2,1)S(1)}, bf16[256,256]{1,0:T(8,128)(2,1)S(1)}, u32[]{:S(2)}, u32[]{:S(2)}) collective-permute-start(bf16[256,256]{1,0:T(8,128)(2,1)S(1)} %get-tuple-element.28), channel_id=1, source_target_pairs={{0,4},{4,0},{8,12},{12,8},{1,5},{5,1},{9,13},{13,9},{2,6},{6,2},{1... | collective-permute-start | bytes 393224 | tf_op jit(solution)/shard_map/ppermute | solution.py:21
  53.5 4.2 %collective-permute-done.11 = bf16[256,256]{1,0:T(8,128)(2,1)S(1)} collective-permute-done((bf16[256,256]{1,0:T(8,128)(2,1)S(1)}, bf16[256,256]{1,0:T(8,128)(2,1)S(1)}, u32[]{:S(2)}, u32[]{:S(2)}) %collective-permute-start.11) | collective-permute-done | bytes 131104 | tf_op jit(solution)/shard_map/ppermute | solution.py:21
  57.7 3.0 %collective-permute-start.12 = (bf16[256,256]{1,0:T(8,128)(2,1)S(1)}, bf16[256,256]{1,0:T(8,128)(2,1)S(1)}, u32[]{:S(2)}, u32[]{:S(2)}) collective-permute-start(bf16[256,256]{1,0:T(8,128)(2,1)S(1)} %add_convert_fusion.1), channel_id=1, source_target_pairs={{0,8},{4,12},{8,0},{12,4},{1,9},{5,13},{9,1},{13,5},{2,10},{6,14},... | collective-permute-start | bytes 393224 | tf_op jit(solution)/shard_map/ppermute | solution.py:21
  60.7 5.3 %collective-permute-done.12 = bf16[256,256]{1,0:T(8,128)(2,1)S(1)} collective-permute-done((bf16[256,256]{1,0:T(8,128)(2,1)S(1)}, bf16[256,256]{1,0:T(8,128)(2,1)S(1)}, u32[]{:S(2)}, u32[]{:S(2)}) %collective-permute-start.12) | collective-permute-done | bytes 131104 | tf_op jit(solution)/shard_map/ppermute | solution.py:21
  66.1 0.7 %fusion = (f32[128,256]{1,0:T(8,128)}, f32[128,256]{1,0:T(8,128)}) fusion(f32[256,256]{1,0:T(8,128)S(1)} %convert_add_fusion), kind=kLoop, calls=%fused_computation.7 | loop fusion | bytes 524288 | tf_op jit(solution)/shard_map/slice | solution.py:304
  (32 shorter events, 2.9 us)
Async XLA Ops:
  0.6 16.4 %copy-start.3 = (bf16[2,64,1024]{2,1,0:T(8,128)(2,1)S(1)}, bf16[2,64,1024]{2,1,0:T(8,128)(2,1)}, u32[]{:S(2)}) copy-start(bf16[2,64,1024]{2,1,0:T(8,128)(2,1)} %param.8) | copy-start | bytes 786436
  1.6 10.5 %collective-permute-start.1 = (bf16[256,256]{1,0:T(8,128)(2,1)S(1)}, bf16[256,256]{1,0:T(8,128)(2,1)S(1)}, u32[]{:S(2)}, u32[]{:S(2)}) collective-permute-start(bf16[256,256]{1,0:T(8,128)(2,1)S(1)} %bitcast.10), channel_id=1, source_target_pairs={{0,8},{4,12},{8,0},{12,4},{1,9},{5,13},{9,1},{13,5},{2,10},{6,14},... | collective-permute-start | bytes 393224 | tf_op jit(solution)/shard_map/ppermute | solution.py:21
  5.7 11.0 %collective-permute-start = (bf16[256,256]{1,0:T(8,128)(2,1)S(1)}, bf16[256,256]{1,0:T(8,128)(2,1)S(1)}, u32[]{:S(2)}, u32[]{:S(2)}) collective-permute-start(bf16[256,256]{1,0:T(8,128)(2,1)S(1)} %bitcast.11), channel_id=1, source_target_pairs={{0,4},{4,0},{8,12},{12,8},{1,5},{5,1},{9,13},{13,9},{2,6},{6,2},{1... | collective-permute-start | bytes 393224 | tf_op jit(solution)/shard_map/ppermute | solution.py:21
  12.1 5.0 %collective-permute-start.2 = (bf16[256,256]{1,0:T(8,128)(2,1)S(1)}, bf16[256,256]{1,0:T(8,128)(2,1)S(1)}, u32[]{:S(2)}, u32[]{:S(2)}) collective-permute-start(bf16[256,256]{1,0:T(8,128)(2,1)S(1)} %collective-permute-done.1.refs_2_), channel_id=1, source_target_pairs={{0,4},{4,0},{8,12},{12,8},{1,5},{5,1},{9,13},{13,9},{2,6},{6,2},{1... | collective-permute-start | bytes 393224 | tf_op jit(solution)/shard_map/ppermute | solution.py:21
  12.7 3.4 %copy-start.2 = (bf16[1024,4096]{1,0:T(8,128)(2,1)S(1)}, bf16[1024,4096]{1,0:T(8,128)(2,1)}, u32[]{:S(2)}) copy-start(bf16[1024,4096]{1,0:T(8,128)(2,1)} %w_ref.1) | copy-start | bytes 25165828
  16.7 3.6 %copy-start = (bf16[1024,4096]{1,0:T(8,128)(2,1)}, bf16[1024,4096]{1,0:T(8,128)(2,1)S(1)}, u32[]{:S(2)}) copy-start(bf16[1024,4096]{1,0:T(8,128)(2,1)S(1)} %hold.1.w_ref) | copy-start | bytes 25165828
  18.5 4.6 %copy-start.6 = (bf16[2,64,1024]{2,1,0:T(8,128)(2,1)S(1)}, bf16[2,64,1024]{2,1,0:T(8,128)(2,1)}, u32[]{:S(2)}) copy-start(bf16[2,64,1024]{2,1,0:T(8,128)(2,1)} %param.12) | copy-start | bytes 786436
  18.5 9.1 %copy-start.7 = (s32[2,64]{1,0:T(2,128)S(1)}, s32[2,64]{1,0:T(2,128)}, u32[]{:S(2)}) copy-start(s32[2,64]{1,0:T(2,128)} %param.13) | copy-start | bytes 1540
  18.5 12.8 %copy-start.4 = (bf16[2,64,1024]{2,1,0:T(8,128)(2,1)S(1)}, bf16[2,64,1024]{2,1,0:T(8,128)(2,1)}, u32[]{:S(2)}) copy-start(bf16[2,64,1024]{2,1,0:T(8,128)(2,1)} %param.11) | copy-start | bytes 786436
  18.5 12.8 %copy-start.5 = (f32[16,1024]{1,0:T(8,128)S(1)}, f32[16,1024]{1,0:T(8,128)}, u32[]{:S(2)}) copy-start(f32[16,1024]{1,0:T(8,128)} %table_ref.1) | copy-start | bytes 196612
  19.0 1.7 %collective-permute-start.5 = (bf16[128,1024]{1,0:T(8,128)(2,1)S(1)}, bf16[128,1024]{1,0:T(8,128)(2,1)S(1)}, u32[]{:S(2)}, u32[]{:S(2)}) collective-permute-start(bf16[128,1024]{1,0:T(8,128)(2,1)S(1)} %project.3), channel_id=1, source_target_pairs={{0,1},{1,0},{2,3},{3,2},{4,5},{5,4},{6,7},{7,6},{8,9},{9,8},{10,11... | collective-permute-start | bytes 786440 | tf_op jit(solution)/shard_map/ppermute | solution.py:21
  20.3 11.6 %collective-permute-start.4 = (bf16[128,1024]{1,0:T(8,128)(2,1)}, bf16[128,1024]{1,0:T(8,128)(2,1)}, u32[]{:S(2)}, u32[]{:S(2)}) collective-permute-start(bf16[128,1024]{1,0:T(8,128)(2,1)} %get-tuple-element.21), channel_id=1, source_target_pairs={{0,1},{1,0},{2,3},{3,2},{4,5},{5,4},{6,7},{7,6},{8,9},{9,8},{10,11... | collective-permute-start | bytes 786440 | tf_op jit(solution)/shard_map/ppermute | solution.py:21
  21.5 10.4 %collective-permute-start.6 = (bf16[128,1024]{1,0:T(8,128)(2,1)}, bf16[128,1024]{1,0:T(8,128)(2,1)}, u32[]{:S(2)}, u32[]{:S(2)}) collective-permute-start(bf16[128,1024]{1,0:T(8,128)(2,1)} %add_convert_fusion), channel_id=1, source_target_pairs={{0,2},{1,3},{2,0},{3,1},{4,6},{5,7},{6,4},{7,5},{8,10},{9,11},{10,... | collective-permute-start | bytes 786440 | tf_op jit(solution)/shard_map/ppermute | solution.py:21
  23.8 7.5 %collective-permute-start.3 = (bf16[64,1024]{1,0:T(8,128)(2,1)}, bf16[64,1024]{1,0:T(8,128)(2,1)S(1)}, u32[]{:S(2)}, u32[]{:S(2)}) collective-permute-start(bf16[64,1024]{1,0:T(8,128)(2,1)} %get-tuple-element.31), channel_id=1, source_target_pairs={{0,12},{4,8},{8,4},{12,0},{1,13},{5,9},{9,5},{13,1},{2,14},{6,10},... | collective-permute-start | bytes 393224 | tf_op jit(solution)/shard_map/ppermute | solution.py:21
  33.2 7.4 %collective-permute-start.8 = (bf16[128,1024]{1,0:T(8,128)(2,1)S(1)}, bf16[128,1024]{1,0:T(8,128)(2,1)S(1)}, u32[]{:S(2)}, u32[]{:S(2)}) collective-permute-start(bf16[128,1024]{1,0:T(8,128)(2,1)S(1)} %multiply_convert_fusion.refs_4_), channel_id=1, source_target_pairs={{0,2},{1,3},{2,0},{3,1},{4,6},{5,7},{6,4},{7,5},{8,10},{9,11},{10,... | collective-permute-start | bytes 786440 | tf_op jit(solution)/shard_map/ppermute | solution.py:21
  33.8 6.8 %collective-permute-start.7 = (bf16[128,1024]{1,0:T(8,128)(2,1)S(1)}, bf16[128,1024]{1,0:T(8,128)(2,1)S(1)}, u32[]{:S(2)}, u32[]{:S(2)}) collective-permute-start(bf16[128,1024]{1,0:T(8,128)(2,1)S(1)} %multiply_convert_fusion.refs_4_), channel_id=1, source_target_pairs={{0,1},{1,0},{2,3},{3,2},{4,5},{5,4},{6,7},{7,6},{8,9},{9,8},{10,11... | collective-permute-start | bytes 786440 | tf_op jit(solution)/shard_map/ppermute | solution.py:21
  40.5 1.5 %collective-permute-start.9 = (bf16[128,1024]{1,0:T(8,128)(2,1)S(1)}, bf16[128,1024]{1,0:T(8,128)(2,1)S(1)}, u32[]{:S(2)}, u32[]{:S(2)}) collective-permute-start(bf16[128,1024]{1,0:T(8,128)(2,1)S(1)} %collective-permute-done.8.refs_6_), channel_id=1, source_target_pairs={{0,1},{1,0},{2,3},{3,2},{4,5},{5,4},{6,7},{7,6},{8,9},{9,8},{10,11... | collective-permute-start | bytes 786440 | tf_op jit(solution)/shard_map/ppermute | solution.py:21
  42.1 3.4 %copy-start.1 = (bf16[1024,4096]{1,0:T(8,128)(2,1)S(1)}, bf16[1024,4096]{1,0:T(8,128)(2,1)}, u32[]{:S(2)}) copy-start(bf16[1024,4096]{1,0:T(8,128)(2,1)} %copy-done) | copy-start | bytes 25165828
  50.5 7.2 %collective-permute-start.11 = (bf16[256,256]{1,0:T(8,128)(2,1)S(1)}, bf16[256,256]{1,0:T(8,128)(2,1)S(1)}, u32[]{:S(2)}, u32[]{:S(2)}) collective-permute-start(bf16[256,256]{1,0:T(8,128)(2,1)S(1)} %get-tuple-element.28), channel_id=1, source_target_pairs={{0,4},{4,0},{8,12},{12,8},{1,5},{5,1},{9,13},{13,9},{2,6},{6,2},{1... | collective-permute-start | bytes 393224 | tf_op jit(solution)/shard_map/ppermute | solution.py:21
  53.4 7.3 %collective-permute-start.10 = (bf16[256,256]{1,0:T(8,128)(2,1)S(1)}, bf16[256,256]{1,0:T(8,128)(2,1)S(1)}, u32[]{:S(2)}, u32[]{:S(2)}) collective-permute-start(bf16[256,256]{1,0:T(8,128)(2,1)S(1)} %get-tuple-element.26), channel_id=1, source_target_pairs={{0,4},{4,0},{8,12},{12,8},{1,5},{5,1},{9,13},{13,9},{2,6},{6,2},{1... | collective-permute-start | bytes 393224 | tf_op jit(solution)/shard_map/ppermute | solution.py:21
  57.7 8.3 %collective-permute-start.12 = (bf16[256,256]{1,0:T(8,128)(2,1)S(1)}, bf16[256,256]{1,0:T(8,128)(2,1)S(1)}, u32[]{:S(2)}, u32[]{:S(2)}) collective-permute-start(bf16[256,256]{1,0:T(8,128)(2,1)S(1)} %add_convert_fusion.1), channel_id=1, source_target_pairs={{0,8},{4,12},{8,0},{12,4},{1,9},{5,13},{9,1},{13,5},{2,10},{6,14},... | collective-permute-start | bytes 393224 | tf_op jit(solution)/shard_map/ppermute | solution.py:21

commit v2 on v1

v2 whole, which is shorter than its diff:
```python
import functools
import math

import jax
import jax.numpy as jnp
from jax import lax
from jax.experimental import pallas as pl
from jax.experimental.pallas import tpu as pltpu
from jax.sharding import PartitionSpec as P

HEAD_DIM = 128
BIG_NEG = -1e30
LOG2E = 1.4426950408889634
F32 = jnp.float32
BF16 = jnp.bfloat16
VMEM = pl.BlockSpec(memory_space=pltpu.VMEM)
ANY = pl.BlockSpec(memory_space=pl.ANY)


def across(block, axis, bit):
    count = lax.axis_size(axis)
    return lax.ppermute(block, axis, [(i, i ^ bit) for i in range(count)])


def bits_of(count):
    return [1 << b for b in range(count.bit_length() - 1)]


def gather_blocks(own, axis, first):
    blocks = {0: own}
    for bit in reversed(bits_of(lax.axis_size(axis))):
        for s in sorted(blocks):
            if s:
                blocks[s], blocks[bit], first = lax.optimization_barrier(
                    (blocks[s], blocks[bit], first)
                )
            blocks[s ^ bit] = [across(b, axis, bit) for b in blocks[s]]
    return [[blocks[s][i] for s in range(len(blocks))] for i in range(len(own))], first


def nt(a, b):
    return lax.dot_general(a, b, (((1,), (1,)), ((), ())), preferred_element_type=F32)


def nn(a, b):
    return jnp.dot(a, b, preferred_element_type=F32)


def call(body, out, args, mib, name, after=(), flops=0):
    count, extra = len(args), len(after)

    def padded(*refs):
        body(*refs[:count], *refs[count + extra :])

    return pl.pallas_call(
        padded,
        out_shape=out,
        in_specs=[VMEM] * count + [ANY] * extra,
        out_specs=jax.tree.map(lambda _: VMEM, out),
        compiler_params=pltpu.CompilerParams(vmem_limit_bytes=mib << 20),
        cost_estimate=cost(flops, 0),
        name=name,
    )(*args, *after)


def cost(flops, moved):
    return pl.CostEstimate(flops=flops, bytes_accessed=moved, transcendentals=0)


def stacked_heads(ref, span, rows, group, per_group):
    pieces = [
        ref[span * rows : (span + 1) * rows, h * HEAD_DIM : (h + 1) * HEAD_DIM]
        for h in range(group * per_group, (group + 1) * per_group)
    ]
    return jnp.concatenate(pieces, axis=0)


def stacked_keys(refs, part, rows, group):
    cols = slice(group * HEAD_DIM, (group + 1) * HEAD_DIM)
    return jnp.concatenate([r[part * rows : (part + 1) * rows, cols] for r in refs], axis=0)


def diagonal_mask(owner_xor, device, rows, columns, upper):
    owner = device ^ owner_xor
    key = lax.broadcasted_iota(jnp.int32, (rows, columns), 0)
    query = lax.broadcasted_iota(jnp.int32, (rows, columns), 1) & (rows - 1)
    ahead = (device - owner if upper else owner - device) * rows
    return key + ahead <= query


def attention_kernel(n, rows, kv_local, per_group, q_ref, *refs):
    k_refs, v_refs, (att_ref, low_ref, high_ref) = refs[:n], refs[n : 2 * n], refs[2 * n :]
    device = lax.axis_index("ctx")
    columns = per_group * rows
    scale = HEAD_DIM**-0.5 * LOG2E
    masks = {
        (s, upper): diagonal_mask(s, device, rows, columns, upper)
        for s in range(n)
        for upper in (False, True)
    }
    for group in range(kv_local):
        keys = [stacked_keys(k_refs, part, rows, group) for part in (0, 1)]
        vals = [stacked_keys(v_refs, part, rows, group) for part in (0, 1)]
        vals_t = [v.astype(F32).T.astype(BF16) for v in vals]
        for span in (0, 1):
            query = stacked_heads(q_ref, span, rows, group, per_group)
            tiles = []
            for half in range(span + 1):
                tile = nt(keys[half], query) * scale
                if half == span:
                    tile = jnp.concatenate(
                        [
                            jnp.where(
                                masks[s, span == 1], tile[s * rows : (s + 1) * rows], BIG_NEG
                            )
                            for s in range(n)
                        ],
                        axis=0,
                    )
                tiles.append(tile)
            top = functools.reduce(
                jnp.maximum, [jnp.max(t, axis=0, keepdims=True) for t in tiles]
            )
            tiles = [jnp.exp2(t - top) for t in tiles]
            total = sum(jnp.sum(t, axis=0, keepdims=True) for t in tiles)
            inverse = 1.0 / total
            mixed = jnp.zeros((HEAD_DIM, columns), F32)
            for half, tile in enumerate(tiles):
                probs = tile * inverse
                if span == 0:
                    low_ref[group] = probs
                else:
                    high_ref[group, half * n * rows : (half + 1) * n * rows] = probs
                mixed += nn(vals_t[half], probs.astype(BF16))
            out = mixed.T.astype(BF16)
            for i in range(per_group):
                h = group * per_group + i
                att_ref[
                    span * rows : (span + 1) * rows, h * HEAD_DIM : (h + 1) * HEAD_DIM
                ] = out[i * rows : (i + 1) * rows]


def project_kernel(width, offsets, a_ref, w_ref, *outs):
    head = lax.axis_index("head")
    for s, out in zip(offsets, outs):
        start = pl.multiple_of((head ^ s) * width, width)
        out[...] = nn(a_ref[...], w_ref[:, pl.ds(start, width)]).astype(out.dtype)


def hold_kernel(w_ref, target_ref, w_out, upper_out, sems):
    copies = [
        pltpu.make_async_copy(target_ref.at[1], upper_out, sems.at[0]),
        pltpu.make_async_copy(w_ref, w_out, sems.at[1]),
    ]
    for copy in copies:
        copy.start()
    for copy in copies:
        copy.wait()


def prepare_kernel(lang_ref, table_ref, residual_ref, target_ref, upper_ref, scale_ref, gap_ref):
    rows = upper_ref.shape[0]
    kinds = table_ref.shape[0]
    for span, target in ((0, target_ref.at[0]), (1, upper_ref)):
        part = slice(span * rows, (span + 1) * rows)
        chosen = lang_ref[span : span + 1] == lax.broadcasted_iota(jnp.int32, (kinds, rows), 0)
        scale_ref[part] = lax.dot_general(
            chosen.astype(F32),
            table_ref[...],
            (((0,), (0,)), ((), ())),
            precision=lax.Precision.HIGHEST,
            preferred_element_type=F32,
        )
        gap_ref[part] = residual_ref[part].astype(F32) - target[...].astype(F32)


def sum_kernel(cut, *refs):
    addends, out = refs[:-1], refs[-1]
    out[...] = sum(a[:, cut].astype(F32) for a in addends).astype(out.dtype)


def gradient_kernel(cut, scale_ref, gap_ref, got_ref, *refs):
    addends, out = refs[:-1], refs[-1]
    scale = scale_ref[:, cut]
    projected = sum((a[:, cut].astype(F32) for a in addends), got_ref[...].astype(F32))
    out[...] = ((gap_ref[:, cut] + projected * scale) * scale).astype(BF16)


def weighted(width, places, g_refs, w_ref):
    head = lax.axis_index("head")
    total = None
    for (s, first, size), g_ref in zip(places, g_refs):
        start = pl.multiple_of((head ^ s) * width + first, size)
        part = nt(g_ref[...], w_ref[:, pl.ds(start, size)])
        total = part if total is None else total + part
    return total


def weighted_kernel(width, places, w_ref, *refs):
    g_refs, (*more, out) = refs[: len(places)], refs[len(places) :]
    total = weighted(width, places, g_refs, w_ref)
    out[...] = total + more[0][...] if more else total


def value_gradient_kernel(n, places, rows, kv_local, per_group, width, *refs):
    w_ref, low_ref, high_ref, more_ref, *refs = refs
    g_refs, (grad_ref, *out_refs) = refs[: len(places)], refs[len(places) :]
    grad = (more_ref[...] + weighted(width, places, g_refs, w_ref)).astype(BF16)
    grad_ref[...] = grad
    for group in range(kv_local):
        cols = slice(group * HEAD_DIM, (group + 1) * HEAD_DIM)
        low_out, high_out = [
            stacked_heads(grad, span, rows, group, per_group) for span in (0, 1)
        ]
        for half in (0, 1):
            part = slice(half * n * rows, (half + 1) * n * rows)
            total = nn(high_ref[group, part].astype(BF16), high_out)
            if half == 0:
                total += nn(low_ref[group].astype(BF16), low_out)
            for s, ref in enumerate(out_refs):
                ref[half * rows : (half + 1) * rows, cols] = total[
                    s * rows : (s + 1) * rows
                ].astype(ref.dtype)


def key_gradient_kernel(n, rows, kv_local, per_group, grad_ref, q_ref, low_ref, high_ref, *refs):
    k_refs, v_refs, (dq_ref, *out_refs) = refs[:n], refs[n : 2 * n], refs[2 * n :]
    columns = per_group * rows
    scale = HEAD_DIM**-0.5
    for group in range(kv_local):
        keys = [stacked_keys(k_refs, part, rows, group) for part in (0, 1)]
        vals = [stacked_keys(v_refs, part, rows, group) for part in (0, 1)]
        keys_t = [k.astype(F32).T.astype(BF16) for k in keys]
        grad_k = [None, None]
        for span in (0, 1):
            query = stacked_heads(q_ref, span, rows, group, per_group)
            out = stacked_heads(grad_ref, span, rows, group, per_group)
            probs = (
                [low_ref[group]]
                if span == 0
                else [high_ref[group, h * n * rows : (h + 1) * n * rows] for h in (0, 1)]
            )
            terms = [p * nt(vals[half], out) for half, p in enumerate(probs)]
            delta = sum(jnp.sum(t, axis=0, keepdims=True) for t in terms)
            grad_q = jnp.zeros((HEAD_DIM, columns), F32)
            for half, (prob, term) in enumerate(zip(probs, terms)):
                step = (term - prob * delta).astype(BF16)
                grad_q += nn(keys_t[half], step)
                dk = nn(step, query)
                grad_k[half] = dk if grad_k[half] is None else grad_k[half] + dk
            grad_q = (grad_q * scale).T
            for i in range(per_group):
                h = group * per_group + i
                dq_ref[span * rows : (span + 1) * rows, h * HEAD_DIM : (h + 1) * HEAD_DIM] = (
                    grad_q[i * rows : (i + 1) * rows]
                )
        cols = slice(group * HEAD_DIM, (group + 1) * HEAD_DIM)
        for half in (0, 1):
            for s, ref in enumerate(out_refs):
                ref[half * rows : (half + 1) * rows, cols] = (
                    grad_k[half][s * rows : (s + 1) * rows] * scale
                ).astype(ref.dtype)


def reduce_blocks(blocks, axis):
    blocks = dict(enumerate(blocks))
    for bit in bits_of(lax.axis_size(axis)):
        for s in sorted((s for s in blocks if s & bit), reverse=True):
            got = across(blocks.pop(s).astype(BF16), axis, bit)
            blocks[s ^ bit] = blocks[s ^ bit].astype(F32) + got.astype(F32)
    return blocks[0]


def on_device(queries, keys, values, residual, targets, lang_ids, lang_scale, out_weight):
    n, nh = lax.axis_size("ctx"), lax.axis_size("head")
    rows = queries.shape[1]
    kv_width, q_width = keys.shape[2], queries.shape[2]
    kv_local, q_local = kv_width // HEAD_DIM, q_width // HEAD_DIM
    per_group = q_local // kv_local
    width = residual.shape[2]
    columns = per_group * rows

    all_rows = 2 * rows
    f32_rows = pltpu.VMEM((all_rows, width), F32)
    flat_q = queries.reshape(all_rows, q_width)
    weight, upper_targets = pl.pallas_call(
        hold_kernel,
        out_shape=(pltpu.VMEM(out_weight.shape, BF16), pltpu.VMEM(targets.shape[1:], BF16)),
        in_specs=[ANY] * 2,
        out_specs=(VMEM, VMEM),
        scratch_shapes=[pltpu.SemaphoreType.DMA((2,))],
        compiler_params=pltpu.CompilerParams(vmem_limit_bytes=50 << 20),
        cost_estimate=cost(0, 4 * math.prod(out_weight.shape)),
        name="hold",
    )(out_weight, targets)
    upper_targets = across(upper_targets, "ctx", n - 1)
    (key_blocks, value_blocks), weight = gather_blocks(
        [keys.reshape(all_rows, kv_width), values.reshape(all_rows, kv_width)], "ctx", weight
    )
    attended, low_probs, high_probs = call(
        functools.partial(attention_kernel, n, rows, kv_local, per_group),
        (
            pltpu.VMEM((all_rows, q_width), BF16),
            pltpu.VMEM((kv_local, n * rows, columns), F32),
            pltpu.VMEM((kv_local, 2 * n * rows, columns), F32),
        ),
        (flat_q, *key_blocks, *value_blocks),
        16,
        "attention",
    )
    row_scales, gap = call(
        prepare_kernel,
        (f32_rows, f32_rows),
        (
            lang_ids,
            lang_scale,
            residual.reshape(all_rows, width),
            targets,
            upper_targets,
        ),
        4,
        "prepare",
        flops=3 << 29,
    )

    half = width // 2
    cuts = [slice(0, half), slice(half, width)]
    bits = bits_of(nh)
    top = bits[-1]
    share = {}

    def project(offsets, after=()):
        for s in offsets:
            block = call(
                functools.partial(project_kernel, width, [s]),
                pltpu.VMEM((all_rows, width), BF16 if s & (top - 1) & 1 else F32),
                (attended, weight),
                8,
                "project",
                after=after,
            )
            share[s] = [block]

    def total(addends, cut, after=()):
        out = pltpu.VMEM((all_rows, cut.stop - cut.start), BF16)
        return call(functools.partial(sum_kernel, cut), out, addends, 4, "sum", after=after)

    def reduce_to(base):
        for bit in bits[:-1]:
            for s in sorted((s for s in share if s & bit and s & top == base), reverse=True):
                addends = share.pop(s)
                whole = total(addends, slice(0, width)) if len(addends) > 1 else addends[0]
                share[s ^ bit].append(across(whole, "head", bit))

    upper_half = range(nh - 1, top - 1, -1)
    firsts = [s for s in upper_half if s & (top - 1) & 1]
    if firsts:
        project(firsts)
    project([s for s in upper_half if s not in firsts])
    reduce_to(top)
    addends = share.pop(top)
    sent = [total(addends, cut, (gap,)) for cut in cuts]
    got = [across(block, "head", top) for block in sent]
    project(range(top - 1, -1, -1), after=sent)
    reduce_to(0)
    blocks = {}
    for c, cut in enumerate(cuts):
        blocks[0, c] = call(
            functools.partial(gradient_kernel, cut),
            pltpu.VMEM((all_rows, half), BF16),
            (row_scales, gap, got[c], *share[0]),
            4,
            "gradient",
        )
        blocks[top, c] = across(blocks[0, c], "head", top)
    for bit in reversed(bits[:-1]):
        for s, c in sorted(blocks):
            blocks[s ^ bit, c] = across(blocks[s, c], "head", bit)
    near = [k for k in sorted(blocks) if k[0] < top]
    far = [(s, 0) for s in range(top, nh)] + [(s, 1) for s in range(top, nh)]
    grad = ()
    for used in (near, far[: top + 1]):
        places = [(s, c * half, half) for s, c in used]
        out = call(
            functools.partial(weighted_kernel, width, places),
            pltpu.VMEM((all_rows, q_width), F32),
            (weight, *(blocks[k] for k in used), *grad),
            8,
            "weighted",
            flops=1 << 31,
        )
        grad = (out,)
    last = far[top + 1 :]
    places = [(s, c * half, half) for s, c in last]
    shares = (
        pltpu.VMEM((all_rows, kv_width), F32),
        *(pltpu.VMEM((all_rows, kv_width), BF16) for _ in range(n - 1)),
    )
    grad_attended, *grad_values = call(
        functools.partial(
            value_gradient_kernel, n, places, rows, kv_local, per_group, width
        ),
        (pltpu.VMEM((all_rows, q_width), BF16), *shares),
        (weight, low_probs, high_probs, *grad, *(blocks[k] for k in last)),
        16,
        "value_gradient",
    )
    grad_queries, *grad_keys = call(
        functools.partial(key_gradient_kernel, n, rows, kv_local, per_group),
        (jax.ShapeDtypeStruct((all_rows, q_width), F32), *shares),
        (grad_attended, flat_q, low_probs, high_probs, *key_blocks, *value_blocks),
        16,
        "key_gradient",
        flops=1 << 31,
    )
    grad_values = reduce_blocks(grad_values, "ctx")
    grad_keys = reduce_blocks(grad_keys, "ctx")
    return (
        grad_queries.reshape(2, rows, q_width),
        grad_keys.reshape(2, rows, kv_width),
        grad_values.reshape(2, rows, kv_width),
    )


def solution(mesh):
    split = P(None, ("groups", "ctx"), "head")
    in_specs = (
        split,
        split,
        split,
        split,
        split,
        P(None, ("groups", "ctx")),
        P(None, "head"),
        P("head", None),
    )
    return jax.shard_map(
        on_device, mesh=mesh, in_specs=in_specs, out_specs=(split, split, split), check_vma=False
    )
```

time: 67.1 us -> 58.1 us (0.87)
  waiting for transfers between devices: 26.7 us -> 15.4 us
  starting transfers between devices: 18.7 us -> 27 us
  local copies, waits for them, and re-layouts: 8.32 us -> 0.04 us
  Pallas kernels: 9.36 us -> 13.3 us
  other arithmetic: 2.98 us -> 1.39 us
    ppermute x13 -> x23, waiting for transfers between devices: 26.7 us -> 15.4 us  [across(): return lax.ppermute(block, axis, [(i, i ^ bit) for i in range(count)])]
    ppermute x13 -> x23, starting transfers between devices: 18.7 us -> 27 us  [across(): return lax.ppermute(block, axis, [(i, i ^ bit) for i in range(count)])]
    unnamed x16 -> x14, local copies, waits for them, and re-layouts: 6.8 us -> 0.04 us
    pallas_call x6 -> x15, Pallas kernels: 9.36 us -> 13.3 us  [the longest x14 9.8 us: call(): pl.pallas_call(padded, out_shape=out, in_specs=[VMEM] * count + [ANY] * e...]
    add x1 -> x2, other arithmetic: 0.04 us -> 1.35 us  [reduce_blocks(): blocks[s ^ bit] = blocks[s ^ bit].astype(F32) + got.astype(F32)]
    convert_element_type x1 -> x0, other arithmetic: 1.21 us -> none  [on_device(): grad_proj = ((gap + projected * row_scales) * row_scales).astype(BF16)]
    concatenate x1 -> x0, other arithmetic: 0.93 us -> none  [on_device(): kv_own = jnp.concatenate([keys, values]).reshape(4 * rows, kv_width)]
    convert_element_type x2, other arithmetic: 0.8 us -> 0.04 us  [reduce_blocks(): got = across(blocks.pop(s).astype(BF16), axis, bit)]
  transfers between devices with their start and end apart: 13 -> 23, of which waited for: 7 -> 11; matrix products, arithmetic and copies ran while one was open for 2% -> 1% of each run, Pallas kernels for 4% -> 21%
where the time goes in v2:
time: 58.1 us; the launch traced here: 58 us
  starting transfers between devices  27 us (46%)
  waiting for transfers between devices  15.4 us (27%)
  Pallas kernels  13.3 us (23%)
  other arithmetic  1.39 us (2%)
  between operations  0.89 us (2%)
    ppermute x23, starting transfers between devices, across(): return lax.ppermute(block, axis, [(i, i ^ bit) for i in range(count)])  27 us
    ppermute x23, waiting for transfers between devices, across(): return lax.ppermute(block, axis, [(i, i ^ bit) for i in range(count)])  15.4 us
    pallas_call x14, Pallas kernels, call(): pl.pallas_call(padded, out_shape=out, in_specs=[VMEM] * count + [ANY] * e...  9.8 us
    pallas_call x1, Pallas kernels, on_device(): pl.pallas_call(hold_kernel, out_shape=(pltpu.VMEM(out_weight.shape, BF16)...  3.48 us
    add x2, other arithmetic, reduce_blocks(): blocks[s ^ bit] = blocks[s ^ bit].astype(F32) + got.astype(F32)  1.35 us
  transfers between devices with their start and end apart: 23, of which 11 were waited for; matrix products, arithmetic and copies ran while one was open for 1% of the time, Pallas kernels for 21%

profile of v2, /device:TPU:0, one launch (start us, length us, event | category | flops | bytes accessed | tf_op | source)
XLA Modules:
  0.0 58.0 jit_solution(8437240052657409372)
XLA Ops:
  0.7 4.1 %collective-permute-start = (bf16[128,256]{1,0:T(8,128)(2,1)}, bf16[128,256]{1,0:T(8,128)(2,1)S(1)}, u32[]{:S(2)}, u32[]{:S(2)}) collective-permute-start(bf16[128,256]{1,0:T(8,128)(2,1)} %bitcast.9), channel_id=1, source_target_pairs={{0,8},{4,12},{8,0},{12,4},{1,9},{5,13},{9,1},{13,5},{2,10},{6,14},... | collective-permute-start | bytes 196616 | tf_op jit(solution)/shard_map/ppermute | solution.py:22
  4.8 1.8 %collective-permute-start.2 = (bf16[128,256]{1,0:T(8,128)(2,1)}, bf16[128,256]{1,0:T(8,128)(2,1)S(1)}, u32[]{:S(2)}, u32[]{:S(2)}) collective-permute-start(bf16[128,256]{1,0:T(8,128)(2,1)} %bitcast.10), channel_id=1, source_target_pairs={{0,4},{4,0},{8,12},{12,8},{1,5},{5,1},{9,13},{13,9},{2,6},{6,2},{1... | collective-permute-start | bytes 196616 | tf_op jit(solution)/shard_map/ppermute | solution.py:22
  6.9 3.5 %hold.1 = (bf16[1024,4096]{1,0:T(8,128)(2,1)S(1)}, bf16[64,1024]{1,0:T(8,128)(2,1)S(1)}) custom-call(bf16[1024,4096]{1,0:T(8,128)(2,1)} %w_ref.1, bf16[2,64,1024]{2,1,0:T(8,128)(2,1)} %refs_3_.1), custom_call_target="tpu_custom_call" | custom-call | bytes 16777216 | tf_op jit(solution)/shard_map/hold/pallas_call | solution.py:286
  12.1 1.0 %collective-permute-start.4 = (bf16[128,256]{1,0:T(8,128)(2,1)S(1)}, bf16[128,256]{1,0:T(8,128)(2,1)S(1)}, u32[]{:S(2)}, u32[]{:S(2)}) collective-permute-start(bf16[128,256]{1,0:T(8,128)(2,1)S(1)} %collective-permute-done.refs_3_.refs_6_), channel_id=1, source_target_pairs={{0,4},{4,0},{8,12},{12,8},{1,5},{5,1},{9,13},{13,9},{2,6},{6,2},{1... | collective-permute-start | bytes 196616 | tf_op jit(solution)/shard_map/ppermute | solution.py:22
  13.0 1.1 %collective-permute-start.5 = (bf16[128,256]{1,0:T(8,128)(2,1)S(1)}, bf16[128,256]{1,0:T(8,128)(2,1)S(1)}, u32[]{:S(2)}, u32[]{:S(2)}) collective-permute-start(bf16[128,256]{1,0:T(8,128)(2,1)S(1)} %collective-permute-done.1.refs_7_.refs_10_), channel_id=1, source_target_pairs={{0,4},{4,0},{8,12},{12,8},{1,5},{5,1},{9,13},{13,9},{2,6},{6,2},{1... | collective-permute-start | bytes 196616 | tf_op jit(solution)/shard_map/ppermute | solution.py:22
  14.1 4.2 %collective-permute-start.6 = (bf16[64,1024]{1,0:T(8,128)(2,1)S(1)}, bf16[64,1024]{1,0:T(8,128)(2,1)S(1)}, u32[]{:S(2)}, u32[]{:S(2)}) collective-permute-start(bf16[64,1024]{1,0:T(8,128)(2,1)S(1)} %get-tuple-element.33), channel_id=1, source_target_pairs={{0,12},{4,8},{8,4},{12,0},{1,13},{5,9},{9,5},{13,1},{2,14},{6,10},... | collective-permute-start | bytes 393224 | tf_op jit(solution)/shard_map/ppermute | solution.py:22
  18.4 1.4 %attention.1 = (bf16[128,1024]{1,0:T(8,128)(2,1)S(1)}, f32[2,256,256]{2,1,0:T(8,128)S(1)}, f32[2,512,256]{2,1,0:T(8,128)S(1)}) custom-call(bf16[128,1024]{1,0:T(8,128)(2,1)S(1)} %bitcast.7, bf16[128,256]{1,0:T(8,128)(2,1)S(1)} %bitcast.11, bf16[128,256]{1,0:T(8,128)(2,1)S(1)} %collective-permute-done.2.refs_2_.refs_5_, ...), custom_call_target="tpu_custom_call" | custom-call | tf_op jit(solution)/shard_map/attention/pallas_call | solution.py:55
  20.9 1.8 %collective-permute-done.6.refs_4_ = bf16[64,1024]{1,0:T(8,128)(2,1)S(1)} collective-permute-done((bf16[64,1024]{1,0:T(8,128)(2,1)S(1)}, bf16[64,1024]{1,0:T(8,128)(2,1)S(1)}, u32[]{:S(2)}, u32[]{:S(2)}) %collective-permute-start.6) | collective-permute-done | bytes 131104 | tf_op jit(solution)/shard_map/ppermute | solution.py:22
  23.9 1.6 %collective-permute-start.8 = (bf16[128,512]{1,0:T(8,128)(2,1)S(1)}, bf16[128,512]{1,0:T(8,128)(2,1)S(1)}, u32[]{:S(2)}, u32[]{:S(2)}) collective-permute-start(bf16[128,512]{1,0:T(8,128)(2,1)S(1)} %sum.2.refs_2_), channel_id=1, source_target_pairs={{0,2},{1,3},{2,0},{3,1},{4,6},{5,7},{6,4},{7,5},{8,10},{9,11},{10,... | collective-permute-start | bytes 393224 | tf_op jit(solution)/shard_map/ppermute | solution.py:22
  26.5 3.8 %collective-permute-done.8.refs_2_ = bf16[128,512]{1,0:T(8,128)(2,1)S(1)} collective-permute-done((bf16[128,512]{1,0:T(8,128)(2,1)S(1)}, bf16[128,512]{1,0:T(8,128)(2,1)S(1)}, u32[]{:S(2)}, u32[]{:S(2)}) %collective-permute-start.8) | collective-permute-done | bytes 131104 | tf_op jit(solution)/shard_map/ppermute | solution.py:22
  30.4 1.6 %collective-permute-start.10 = (bf16[128,512]{1,0:T(8,128)(2,1)S(1)}, bf16[128,512]{1,0:T(8,128)(2,1)S(1)}, u32[]{:S(2)}, u32[]{:S(2)}) collective-permute-start(bf16[128,512]{1,0:T(8,128)(2,1)S(1)} %gradient.2.refs_1_), channel_id=1, source_target_pairs={{0,2},{1,3},{2,0},{3,1},{4,6},{5,7},{6,4},{7,5},{8,10},{9,11},{10,... | collective-permute-start | bytes 393224 | tf_op jit(solution)/shard_map/ppermute | solution.py:22
  31.9 1.1 %collective-permute-done.12.refs_2_ = bf16[128,512]{1,0:T(8,128)(2,1)S(1)} collective-permute-done((bf16[128,512]{1,0:T(8,128)(2,1)S(1)}, bf16[128,512]{1,0:T(8,128)(2,1)S(1)}, u32[]{:S(2)}, u32[]{:S(2)}) %collective-permute-start.12) | collective-permute-done | bytes 131104 | tf_op jit(solution)/shard_map/ppermute | solution.py:22
  33.1 1.6 %collective-permute-start.13 = (bf16[128,512]{1,0:T(8,128)(2,1)S(1)}, bf16[128,512]{1,0:T(8,128)(2,1)S(1)}, u32[]{:S(2)}, u32[]{:S(2)}) collective-permute-start(bf16[128,512]{1,0:T(8,128)(2,1)S(1)} %gradient.3.refs_2_), channel_id=1, source_target_pairs={{0,2},{1,3},{2,0},{3,1},{4,6},{5,7},{6,4},{7,5},{8,10},{9,11},{10,... | collective-permute-start | bytes 393224 | tf_op jit(solution)/shard_map/ppermute | solution.py:22
  35.1 0.7 %collective-permute-done.10.refs_1_ = bf16[128,512]{1,0:T(8,128)(2,1)S(1)} collective-permute-done((bf16[128,512]{1,0:T(8,128)(2,1)S(1)}, bf16[128,512]{1,0:T(8,128)(2,1)S(1)}, u32[]{:S(2)}, u32[]{:S(2)}) %collective-permute-start.10) | collective-permute-done | bytes 131104 | tf_op jit(solution)/shard_map/ppermute | solution.py:22
  35.9 2.4 %collective-permute-done.13.refs_3_ = bf16[128,512]{1,0:T(8,128)(2,1)S(1)} collective-permute-done((bf16[128,512]{1,0:T(8,128)(2,1)S(1)}, bf16[128,512]{1,0:T(8,128)(2,1)S(1)}, u32[]{:S(2)}, u32[]{:S(2)}) %collective-permute-start.13) | collective-permute-done | bytes 131104 | tf_op jit(solution)/shard_map/ppermute | solution.py:22
  38.3 1.5 %weighted.2.refs_4_ = f32[128,1024]{1,0:T(8,128)S(1)} custom-call(bf16[1024,4096]{1,0:T(8,128)(2,1)S(1)} %get-tuple-element.26.refs_1_.refs_0_, bf16[128,512]{1,0:T(8,128)(2,1)S(1)} %gradient.2.refs_1_, bf16[128,512]{1,0:T(8,128)(2,1)S(1)} %gradient.3.refs_2_, bf16[128,512]{1,0:T(8,128)(2,1)S(1)} %collective-permute-done.14.refs_3_, ...), custom_call_target="tpu_custom_call" | custom-call | flops 2147483648 | tf_op jit(solution)/shard_map/weighted/pallas_call | solution.py:55
  39.8 1.2 %weighted.3.refs_3_ = f32[128,1024]{1,0:T(8,128)S(1)} custom-call(bf16[1024,4096]{1,0:T(8,128)(2,1)S(1)} %get-tuple-element.26.refs_1_.refs_0_, bf16[128,512]{1,0:T(8,128)(2,1)S(1)} %collective-permute-done.10.refs_1_, bf16[128,512]{1,0:T(8,128)(2,1)S(1)} %collective-permute-done.11.refs_2_, bf16[128,512]{1,0:T(8,128)(2,1)S(1)} %collective-permute-done.13.refs_3_, ...), custom_call_target="tpu_custom_call" | custom-call | flops 2147483648 | tf_op jit(solution)/shard_map/weighted/pallas_call | solution.py:55
  41.0 0.7 %value_gradient.1 = (bf16[128,1024]{1,0:T(8,128)(2,1)S(1)}, f32[128,256]{1,0:T(8,128)S(1)}, bf16[128,256]{1,0:T(8,128)(2,1)S(1)}, bf16[128,256]{1,0:T(8,128)(2,1)S(1)}, bf16[128,256]{1,0:T(8,128)(2,1)S(1)}) custom-call(bf16[1024,4096]{1,0:T(8,128)(2,1)S(1)} %get-tuple-element.26.refs_1_.refs_0_, f32[2,256,256]{2,1,0:T(8,128)S(1)} %get-tuple-element.31.refs_1_.refs_2_, ...), custom_call_target="tpu_custom_call" | custom-call | tf_op jit(solution)/shard_map/value_gradient/pallas_call | solution.py:55
  42.3 1.5 %collective-permute-start.20 = (bf16[128,256]{1,0:T(8,128)(2,1)S(1)}, bf16[128,256]{1,0:T(8,128)(2,1)S(1)}, u32[]{:S(2)}, u32[]{:S(2)}) collective-permute-start(bf16[128,256]{1,0:T(8,128)(2,1)S(1)} %get-tuple-element.44), channel_id=1, source_target_pairs={{0,4},{4,0},{8,12},{12,8},{1,5},{5,1},{9,13},{13,9},{2,6},{6,2},{1... | collective-permute-start | bytes 196616 | tf_op jit(solution)/shard_map/ppermute | solution.py:22
  43.8 2.3 %key_gradient.1 = (f32[128,1024]{1,0:T(8,128)}, f32[128,256]{1,0:T(8,128)S(1)}, bf16[128,256]{1,0:T(8,128)(2,1)S(1)}, bf16[128,256]{1,0:T(8,128)(2,1)S(1)}, bf16[128,256]{1,0:T(8,128)(2,1)S(1)}) custom-call(bf16[128,1024]{1,0:T(8,128)(2,1)S(1)} %get-tuple-element.37.refs_0_, bf16[128,1024]{1,0:T(8,128)(2,1)S(1)} %bitcast.8, ...), custom_call_target="tpu_custom_call" | custom-call | flops 2147483648 | tf_op jit(solution)/shard_map/key_gradient/pallas_call | solution.py:55
  46.7 1.5 %collective-permute-start.17 = (bf16[128,256]{1,0:T(8,128)(2,1)S(1)}, bf16[128,256]{1,0:T(8,128)(2,1)S(1)}, u32[]{:S(2)}, u32[]{:S(2)}) collective-permute-start(bf16[128,256]{1,0:T(8,128)(2,1)S(1)} %get-tuple-element.40), channel_id=1, source_target_pairs={{0,4},{4,0},{8,12},{12,8},{1,5},{5,1},{9,13},{13,9},{2,6},{6,2},{1... | collective-permute-start | bytes 196616 | tf_op jit(solution)/shard_map/ppermute | solution.py:22
  48.2 2.1 %collective-permute-start.22 = (bf16[128,256]{1,0:T(8,128)(2,1)S(1)}, bf16[128,256]{1,0:T(8,128)(2,1)S(1)}, u32[]{:S(2)}, u32[]{:S(2)}) collective-permute-start(bf16[128,256]{1,0:T(8,128)(2,1)S(1)} %add_convert_fusion), channel_id=1, source_target_pairs={{0,8},{4,12},{8,0},{12,4},{1,9},{5,13},{9,1},{13,5},{2,10},{6,14},... | collective-permute-start | bytes 196616 | tf_op jit(solution)/shard_map/ppermute | solution.py:22
  50.8 2.4 %collective-permute-start.19 = (bf16[128,256]{1,0:T(8,128)(2,1)S(1)}, bf16[128,256]{1,0:T(8,128)(2,1)S(1)}, u32[]{:S(2)}, u32[]{:S(2)}) collective-permute-start(bf16[128,256]{1,0:T(8,128)(2,1)S(1)} %add_convert_fusion.1), channel_id=1, source_target_pairs={{0,8},{4,12},{8,0},{12,4},{1,9},{5,13},{9,1},{13,5},{2,10},{6,14},... | collective-permute-start | bytes 196616 | tf_op jit(solution)/shard_map/ppermute | solution.py:22
  53.2 3.3 %collective-permute-done.22 = bf16[128,256]{1,0:T(8,128)(2,1)S(1)} collective-permute-done((bf16[128,256]{1,0:T(8,128)(2,1)S(1)}, bf16[128,256]{1,0:T(8,128)(2,1)S(1)}, u32[]{:S(2)}, u32[]{:S(2)}) %collective-permute-start.22) | collective-permute-done | bytes 65568 | tf_op jit(solution)/shard_map/ppermute | solution.py:22
  (55 shorter events, 9.1 us)
Async XLA Ops:
  0.6 17.7 %copy-start.2 = (bf16[2,64,256]{2,1,0:T(8,128)(2,1)S(1)}, bf16[2,64,256]{2,1,0:T(8,128)(2,1)}, u32[]{:S(2)}) copy-start(bf16[2,64,256]{2,1,0:T(8,128)(2,1)} %param.9) | copy-start | bytes 196612
  0.7 9.7 %collective-permute-start = (bf16[128,256]{1,0:T(8,128)(2,1)}, bf16[128,256]{1,0:T(8,128)(2,1)S(1)}, u32[]{:S(2)}, u32[]{:S(2)}) collective-permute-start(bf16[128,256]{1,0:T(8,128)(2,1)} %bitcast.9), channel_id=1, source_target_pairs={{0,8},{4,12},{8,0},{12,4},{1,9},{5,13},{9,1},{13,5},{2,10},{6,14},... | collective-permute-start | bytes 196616 | tf_op jit(solution)/shard_map/ppermute | solution.py:22
  4.8 6.3 %collective-permute-start.1 = (bf16[128,256]{1,0:T(8,128)(2,1)}, bf16[128,256]{1,0:T(8,128)(2,1)S(1)}, u32[]{:S(2)}, u32[]{:S(2)}) collective-permute-start(bf16[128,256]{1,0:T(8,128)(2,1)} %bitcast.13), channel_id=1, source_target_pairs={{0,8},{4,12},{8,0},{12,4},{1,9},{5,13},{9,1},{13,5},{2,10},{6,14},... | collective-permute-start | bytes 196616 | tf_op jit(solution)/shard_map/ppermute | solution.py:22
  4.8 6.5 %collective-permute-start.2 = (bf16[128,256]{1,0:T(8,128)(2,1)}, bf16[128,256]{1,0:T(8,128)(2,1)S(1)}, u32[]{:S(2)}, u32[]{:S(2)}) collective-permute-start(bf16[128,256]{1,0:T(8,128)(2,1)} %bitcast.10), channel_id=1, source_target_pairs={{0,4},{4,0},{8,12},{12,8},{1,5},{5,1},{9,13},{13,9},{2,6},{6,2},{1... | collective-permute-start | bytes 196616 | tf_op jit(solution)/shard_map/ppermute | solution.py:22
  6.7 5.4 %collective-permute-start.3 = (bf16[128,256]{1,0:T(8,128)(2,1)}, bf16[128,256]{1,0:T(8,128)(2,1)S(1)}, u32[]{:S(2)}, u32[]{:S(2)}) collective-permute-start(bf16[128,256]{1,0:T(8,128)(2,1)} %bitcast.14), channel_id=1, source_target_pairs={{0,4},{4,0},{8,12},{12,8},{1,5},{5,1},{9,13},{13,9},{2,6},{6,2},{1... | collective-permute-start | bytes 196616 | tf_op jit(solution)/shard_map/ppermute | solution.py:22
  12.1 6.3 %collective-permute-start.4 = (bf16[128,256]{1,0:T(8,128)(2,1)S(1)}, bf16[128,256]{1,0:T(8,128)(2,1)S(1)}, u32[]{:S(2)}, u32[]{:S(2)}) collective-permute-start(bf16[128,256]{1,0:T(8,128)(2,1)S(1)} %collective-permute-done.refs_3_.refs_6_), channel_id=1, source_target_pairs={{0,4},{4,0},{8,12},{12,8},{1,5},{5,1},{9,13},{13,9},{2,6},{6,2},{1... | collective-permute-start | bytes 196616 | tf_op jit(solution)/shard_map/ppermute | solution.py:22
  13.0 5.3 %collective-permute-start.5 = (bf16[128,256]{1,0:T(8,128)(2,1)S(1)}, bf16[128,256]{1,0:T(8,128)(2,1)S(1)}, u32[]{:S(2)}, u32[]{:S(2)}) collective-permute-start(bf16[128,256]{1,0:T(8,128)(2,1)S(1)} %collective-permute-done.1.refs_7_.refs_10_), channel_id=1, source_target_pairs={{0,4},{4,0},{8,12},{12,8},{1,5},{5,1},{9,13},{13,9},{2,6},{6,2},{1... | collective-permute-start | bytes 196616 | tf_op jit(solution)/shard_map/ppermute | solution.py:22
  14.1 8.6 %collective-permute-start.6 = (bf16[64,1024]{1,0:T(8,128)(2,1)S(1)}, bf16[64,1024]{1,0:T(8,128)(2,1)S(1)}, u32[]{:S(2)}, u32[]{:S(2)}) collective-permute-start(bf16[64,1024]{1,0:T(8,128)(2,1)S(1)} %get-tuple-element.33), channel_id=1, source_target_pairs={{0,12},{4,8},{8,4},{12,0},{1,13},{5,9},{9,5},{13,1},{2,14},{6,10},... | collective-permute-start | bytes 393224 | tf_op jit(solution)/shard_map/ppermute | solution.py:22
  20.3 3.0 %collective-permute-start.7 = (bf16[128,1024]{1,0:T(8,128)(2,1)S(1)}, bf16[128,1024]{1,0:T(8,128)(2,1)S(1)}, u32[]{:S(2)}, u32[]{:S(2)}) collective-permute-start(bf16[128,1024]{1,0:T(8,128)(2,1)S(1)} %project.5), channel_id=1, source_target_pairs={{0,1},{1,0},{2,3},{3,2},{4,5},{5,4},{6,7},{7,6},{8,9},{9,8},{10,11... | collective-permute-start | bytes 786440 | tf_op jit(solution)/shard_map/ppermute | solution.py:22
  23.8 6.4 %collective-permute-start.9 = (bf16[128,1024]{1,0:T(8,128)(2,1)S(1)}, bf16[128,1024]{1,0:T(8,128)(2,1)S(1)}, u32[]{:S(2)}, u32[]{:S(2)}) collective-permute-start(bf16[128,1024]{1,0:T(8,128)(2,1)S(1)} %project.7), channel_id=1, source_target_pairs={{0,1},{1,0},{2,3},{3,2},{4,5},{5,4},{6,7},{7,6},{8,9},{9,8},{10,11... | collective-permute-start | bytes 786440 | tf_op jit(solution)/shard_map/ppermute | solution.py:22
  23.9 6.4 %collective-permute-start.8 = (bf16[128,512]{1,0:T(8,128)(2,1)S(1)}, bf16[128,512]{1,0:T(8,128)(2,1)S(1)}, u32[]{:S(2)}, u32[]{:S(2)}) collective-permute-start(bf16[128,512]{1,0:T(8,128)(2,1)S(1)} %sum.2.refs_2_), channel_id=1, source_target_pairs={{0,2},{1,3},{2,0},{3,1},{4,6},{5,7},{6,4},{7,5},{8,10},{9,11},{10,... | collective-permute-start | bytes 393224 | tf_op jit(solution)/shard_map/ppermute | solution.py:22
  25.5 7.5 %collective-permute-start.12 = (bf16[128,512]{1,0:T(8,128)(2,1)S(1)}, bf16[128,512]{1,0:T(8,128)(2,1)S(1)}, u32[]{:S(2)}, u32[]{:S(2)}) collective-permute-start(bf16[128,512]{1,0:T(8,128)(2,1)S(1)} %sum.3.refs_3_), channel_id=1, source_target_pairs={{0,2},{1,3},{2,0},{3,1},{4,6},{5,7},{6,4},{7,5},{8,10},{9,11},{10,... | collective-permute-start | bytes 393224 | tf_op jit(solution)/shard_map/ppermute | solution.py:22
  30.4 5.5 %collective-permute-start.10 = (bf16[128,512]{1,0:T(8,128)(2,1)S(1)}, bf16[128,512]{1,0:T(8,128)(2,1)S(1)}, u32[]{:S(2)}, u32[]{:S(2)}) collective-permute-start(bf16[128,512]{1,0:T(8,128)(2,1)S(1)} %gradient.2.refs_1_), channel_id=1, source_target_pairs={{0,2},{1,3},{2,0},{3,1},{4,6},{5,7},{6,4},{7,5},{8,10},{9,11},{10,... | collective-permute-start | bytes 393224 | tf_op jit(solution)/shard_map/ppermute | solution.py:22
  33.1 5.2 %collective-permute-start.13 = (bf16[128,512]{1,0:T(8,128)(2,1)S(1)}, bf16[128,512]{1,0:T(8,128)(2,1)S(1)}, u32[]{:S(2)}, u32[]{:S(2)}) collective-permute-start(bf16[128,512]{1,0:T(8,128)(2,1)S(1)} %gradient.3.refs_2_), channel_id=1, source_target_pairs={{0,2},{1,3},{2,0},{3,1},{4,6},{5,7},{6,4},{7,5},{8,10},{9,11},{10,... | collective-permute-start | bytes 393224 | tf_op jit(solution)/shard_map/ppermute | solution.py:22
  34.6 3.6 %collective-permute-start.15 = (bf16[128,512]{1,0:T(8,128)(2,1)S(1)}, bf16[128,512]{1,0:T(8,128)(2,1)S(1)}, u32[]{:S(2)}, u32[]{:S(2)}) collective-permute-start(bf16[128,512]{1,0:T(8,128)(2,1)S(1)} %gradient.3.refs_2_), channel_id=1, source_target_pairs={{0,1},{1,0},{2,3},{3,2},{4,5},{5,4},{6,7},{7,6},{8,9},{9,8},{10,11... | collective-permute-start | bytes 393224 | tf_op jit(solution)/shard_map/ppermute | solution.py:22
  34.6 3.6 %collective-permute-start.14 = (bf16[128,512]{1,0:T(8,128)(2,1)S(1)}, bf16[128,512]{1,0:T(8,128)(2,1)S(1)}, u32[]{:S(2)}, u32[]{:S(2)}) collective-permute-start(bf16[128,512]{1,0:T(8,128)(2,1)S(1)} %gradient.2.refs_1_), channel_id=1, source_target_pairs={{0,1},{1,0},{2,3},{3,2},{4,5},{5,4},{6,7},{7,6},{8,9},{9,8},{10,11... | collective-permute-start | bytes 393224 | tf_op jit(solution)/shard_map/ppermute | solution.py:22
  35.9 3.9 %collective-permute-start.11 = (bf16[128,512]{1,0:T(8,128)(2,1)S(1)}, bf16[128,512]{1,0:T(8,128)(2,1)S(1)}, u32[]{:S(2)}, u32[]{:S(2)}) collective-permute-start(bf16[128,512]{1,0:T(8,128)(2,1)S(1)} %collective-permute-done.10.refs_1_), channel_id=1, source_target_pairs={{0,1},{1,0},{2,3},{3,2},{4,5},{5,4},{6,7},{7,6},{8,9},{9,8},{10,11... | collective-permute-start | bytes 393224 | tf_op jit(solution)/shard_map/ppermute | solution.py:22
  38.3 2.7 %collective-permute-start.16 = (bf16[128,512]{1,0:T(8,128)(2,1)S(1)}, bf16[128,512]{1,0:T(8,128)(2,1)S(1)}, u32[]{:S(2)}, u32[]{:S(2)}) collective-permute-start(bf16[128,512]{1,0:T(8,128)(2,1)S(1)} %collective-permute-done.13.refs_3_), channel_id=1, source_target_pairs={{0,1},{1,0},{2,3},{3,2},{4,5},{5,4},{6,7},{7,6},{8,9},{9,8},{10,11... | collective-permute-start | bytes 393224 | tf_op jit(solution)/shard_map/ppermute | solution.py:22
  41.7 6.4 %collective-permute-start.21 = (bf16[128,256]{1,0:T(8,128)(2,1)S(1)}, bf16[128,256]{1,0:T(8,128)(2,1)S(1)}, u32[]{:S(2)}, u32[]{:S(2)}) collective-permute-start(bf16[128,256]{1,0:T(8,128)(2,1)S(1)} %get-tuple-element.46), channel_id=1, source_target_pairs={{0,4},{4,0},{8,12},{12,8},{1,5},{5,1},{9,13},{13,9},{2,6},{6,2},{1... | collective-permute-start | bytes 196616 | tf_op jit(solution)/shard_map/ppermute | solution.py:22
  42.3 10.9 %collective-permute-start.20 = (bf16[128,256]{1,0:T(8,128)(2,1)S(1)}, bf16[128,256]{1,0:T(8,128)(2,1)S(1)}, u32[]{:S(2)}, u32[]{:S(2)}) collective-permute-start(bf16[128,256]{1,0:T(8,128)(2,1)S(1)} %get-tuple-element.44), channel_id=1, source_target_pairs={{0,4},{4,0},{8,12},{12,8},{1,5},{5,1},{9,13},{13,9},{2,6},{6,2},{1... | collective-permute-start | bytes 196616 | tf_op jit(solution)/shard_map/ppermute | solution.py:22
  46.1 4.6 %collective-permute-start.18 = (bf16[128,256]{1,0:T(8,128)(2,1)S(1)}, bf16[128,256]{1,0:T(8,128)(2,1)S(1)}, u32[]{:S(2)}, u32[]{:S(2)}) collective-permute-start(bf16[128,256]{1,0:T(8,128)(2,1)S(1)} %get-tuple-element.42), channel_id=1, source_target_pairs={{0,4},{4,0},{8,12},{12,8},{1,5},{5,1},{9,13},{13,9},{2,6},{6,2},{1... | collective-permute-start | bytes 196616 | tf_op jit(solution)/shard_map/ppermute | solution.py:22
  46.7 10.5 %collective-permute-start.17 = (bf16[128,256]{1,0:T(8,128)(2,1)S(1)}, bf16[128,256]{1,0:T(8,128)(2,1)S(1)}, u32[]{:S(2)}, u32[]{:S(2)}) collective-permute-start(bf16[128,256]{1,0:T(8,128)(2,1)S(1)} %get-tuple-element.40), channel_id=1, source_target_pairs={{0,4},{4,0},{8,12},{12,8},{1,5},{5,1},{9,13},{13,9},{2,6},{6,2},{1... | collective-permute-start | bytes 196616 | tf_op jit(solution)/shard_map/ppermute | solution.py:22
  48.2 8.3 %collective-permute-start.22 = (bf16[128,256]{1,0:T(8,128)(2,1)S(1)}, bf16[128,256]{1,0:T(8,128)(2,1)S(1)}, u32[]{:S(2)}, u32[]{:S(2)}) collective-permute-start(bf16[128,256]{1,0:T(8,128)(2,1)S(1)} %add_convert_fusion), channel_id=1, source_target_pairs={{0,8},{4,12},{8,0},{12,4},{1,9},{5,13},{9,1},{13,5},{2,10},{6,14},... | collective-permute-start | bytes 196616 | tf_op jit(solution)/shard_map/ppermute | solution.py:22
  50.8 6.5 %collective-permute-start.19 = (bf16[128,256]{1,0:T(8,128)(2,1)S(1)}, bf16[128,256]{1,0:T(8,128)(2,1)S(1)}, u32[]{:S(2)}, u32[]{:S(2)}) collective-permute-start(bf16[128,256]{1,0:T(8,128)(2,1)S(1)} %add_convert_fusion.1), channel_id=1, source_target_pairs={{0,8},{4,12},{8,0},{12,4},{1,9},{5,13},{9,1},{13,5},{2,10},{6,14},... | collective-permute-start | bytes 196616 | tf_op jit(solution)/shard_map/ppermute | solution.py:22
  (6 other events, 46.7 us)

commit v3 on v2

--- a/solution.py
+++ b/solution.py
@@ -13,6 +13,7 @@
 LOG2E = 1.4426950408889634
 F32 = jnp.float32
 BF16 = jnp.bfloat16
+PREPARE, SPREAD, KEYS, QUERIES, PROJECT, SECOND = 3 << 31, 1 << 31, 1 << 31, 1 << 31, 1 << 28, 1 << 30
 VMEM = pl.BlockSpec(memory_space=pltpu.VMEM)
 ANY = pl.BlockSpec(memory_space=pl.ANY)
 
@@ -31,9 +32,9 @@
     for bit in reversed(bits_of(lax.axis_size(axis))):
         for s in sorted(blocks):
             if s:
-                blocks[s], blocks[bit], first = lax.optimization_barrier(
-                    (blocks[s], blocks[bit], first)
-                )
+                ahead, *others = blocks[s]
+                ahead, first = lax.optimization_barrier((ahead, first))
+                blocks[s] = [ahead, *others]
             blocks[s ^ bit] = [across(b, axis, bit) for b in blocks[s]]
     return [[blocks[s][i] for s in range(len(blocks))] for i in range(len(own))], first
 
@@ -98,41 +99,36 @@
         for s in range(n)
         for upper in (False, True)
     }
+    part = n * rows
+    stores = (low_ref, high_ref)
     for group in range(kv_local):
-        keys = [stacked_keys(k_refs, part, rows, group) for part in (0, 1)]
-        vals = [stacked_keys(v_refs, part, rows, group) for part in (0, 1)]
-        vals_t = [v.astype(F32).T.astype(BF16) for v in vals]
+        keys = [stacked_keys(k_refs, half, rows, group) for half in (0, 1)]
         for span in (0, 1):
             query = stacked_heads(q_ref, span, rows, group, per_group)
-            tiles = []
             for half in range(span + 1):
                 tile = nt(keys[half], query) * scale
-                if half == span:
-                    tile = jnp.concatenate(
-                        [
-                            jnp.where(
-                                masks[s, span == 1], tile[s * rows : (s + 1) * rows], BIG_NEG
-                            )
-                            for s in range(n)
-                        ],
-                        axis=0,
-                    )
-                tiles.append(tile)
+                for s in range(n):
+                    block = tile[s * rows : (s + 1) * rows]
+                    if half == span:
+                        block = jnp.where(masks[s, span == 1], block, BIG_NEG)
+                    first = half * part + s * rows
+                    stores[span][group, first : first + rows] = block
+    for group in range(kv_local):
+        vals_t = [stacked_keys(v_refs, half, rows, group).T for half in (0, 1)]
+        for span in (0, 1):
+            store = stores[span]
+            tiles = [store[group, h * part : (h + 1) * part] for h in range(span + 1)]
             top = functools.reduce(
                 jnp.maximum, [jnp.max(t, axis=0, keepdims=True) for t in tiles]
             )
             tiles = [jnp.exp2(t - top) for t in tiles]
-            total = sum(jnp.sum(t, axis=0, keepdims=True) for t in tiles)
-            inverse = 1.0 / total
+            inverse = 1.0 / sum(jnp.sum(t, axis=0, keepdims=True) for t in tiles)
             mixed = jnp.zeros((HEAD_DIM, columns), F32)
             for half, tile in enumerate(tiles):
                 probs = tile * inverse
-                if span == 0:
-                    low_ref[group] = probs
-                else:
-                    high_ref[group, half * n * rows : (half + 1) * n * rows] = probs
+                store[group, half * part : (half + 1) * part] = probs
                 mixed += nn(vals_t[half], probs.astype(BF16))
-            out = mixed.T.astype(BF16)
+            out = mixed.astype(BF16).T
             for i in range(per_group):
                 h = group * per_group + i
                 att_ref[
@@ -140,11 +136,10 @@
                 ] = out[i * rows : (i + 1) * rows]
 
 
-def project_kernel(width, offsets, a_ref, w_ref, *outs):
-    head = lax.axis_index("head")
-    for s, out in zip(offsets, outs):
-        start = pl.multiple_of((head ^ s) * width, width)
-        out[...] = nn(a_ref[...], w_ref[:, pl.ds(start, width)]).astype(out.dtype)
+def project_kernel(width, s, cut, a_ref, w_ref, out_ref):
+    size = cut.stop - cut.start
+    start = pl.multiple_of((lax.axis_index("head") ^ s) * width + cut.start, size)
+    out_ref[...] = nn(a_ref[...], w_ref[:, pl.ds(start, size)]).astype(out_ref.dtype)
 
 
 def hold_kernel(w_ref, target_ref, w_out, upper_out, sems):
@@ -174,9 +169,9 @@
         gap_ref[part] = residual_ref[part].astype(F32) - target[...].astype(F32)
 
 
-def sum_kernel(cut, *refs):
+def sum_kernel(*refs):
     addends, out = refs[:-1], refs[-1]
-    out[...] = sum(a[:, cut].astype(F32) for a in addends).astype(out.dtype)
+    out[...] = sum(a[...].astype(F32) for a in addends).astype(out.dtype)
 
 
 def gradient_kernel(cut, scale_ref, gap_ref, got_ref, *refs):
@@ -224,51 +219,61 @@
 
 
 def key_gradient_kernel(n, rows, kv_local, per_group, grad_ref, q_ref, low_ref, high_ref, *refs):
-    k_refs, v_refs, (dq_ref, *out_refs) = refs[:n], refs[n : 2 * n], refs[2 * n :]
-    columns = per_group * rows
-    scale = HEAD_DIM**-0.5
+    v_refs, (low_step_ref, high_step_ref, *out_refs) = refs[:n], refs[n:]
+    part = n * rows
     for group in range(kv_local):
-        keys = [stacked_keys(k_refs, part, rows, group) for part in (0, 1)]
-        vals = [stacked_keys(v_refs, part, rows, group) for part in (0, 1)]
-        keys_t = [k.astype(F32).T.astype(BF16) for k in keys]
+        vals = [stacked_keys(v_refs, half, rows, group) for half in (0, 1)]
         grad_k = [None, None]
         for span in (0, 1):
             query = stacked_heads(q_ref, span, rows, group, per_group)
             out = stacked_heads(grad_ref, span, rows, group, per_group)
-            probs = (
-                [low_ref[group]]
-                if span == 0
-                else [high_ref[group, h * n * rows : (h + 1) * n * rows] for h in (0, 1)]
-            )
+            prob_ref, step_ref = (low_ref, low_step_ref) if span == 0 else (high_ref, high_step_ref)
+            probs = [prob_ref[group, h * part : (h + 1) * part] for h in range(span + 1)]
             terms = [p * nt(vals[half], out) for half, p in enumerate(probs)]
             delta = sum(jnp.sum(t, axis=0, keepdims=True) for t in terms)
-            grad_q = jnp.zeros((HEAD_DIM, columns), F32)
             for half, (prob, term) in enumerate(zip(probs, terms)):
                 step = (term - prob * delta).astype(BF16)
-                grad_q += nn(keys_t[half], step)
+                step_ref[group, half * part : (half + 1) * part] = step
                 dk = nn(step, query)
                 grad_k[half] = dk if grad_k[half] is None else grad_k[half] + dk
+        cols = slice(group * HEAD_DIM, (group + 1) * HEAD_DIM)
+        scale = HEAD_DIM**-0.5
+        for half in (0, 1):
+            for s, ref in enumerate(out_refs):
+                ref[half * rows : (half + 1) * rows, cols] = (
+                    grad_k[half][s * rows : (s + 1) * rows] * scale
+                ).astype(ref.dtype)
+
+
+def query_gradient_kernel(n, rows, kv_local, per_group, low_ref, high_ref, *refs):
+    k_refs, dq_ref = refs[:n], refs[n]
+    part = n * rows
+    scale = HEAD_DIM**-0.5
+    for group in range(kv_local):
+        keys_t = [
+            stacked_keys(k_refs, half, rows, group).astype(F32).T.astype(BF16) for half in (0, 1)
+        ]
+        for span, step_ref in ((0, low_ref), (1, high_ref)):
+            grad_q = sum(
+                nn(keys_t[half], step_ref[group, half * part : (half + 1) * part])
+                for half in range(span + 1)
+            )
             grad_q = (grad_q * scale).T
             for i in range(per_group):
                 h = group * per_group + i
                 dq_ref[span * rows : (span + 1) * rows, h * HEAD_DIM : (h + 1) * HEAD_DIM] = (
                     grad_q[i * rows : (i + 1) * rows]
                 )
-        cols = slice(group * HEAD_DIM, (group + 1) * HEAD_DIM)
-        for half in (0, 1):
-            for s, ref in enumerate(out_refs):
-                ref[half * rows : (half + 1) * rows, cols] = (
-                    grad_k[half][s * rows : (s + 1) * rows] * scale
-                ).astype(ref.dtype)
 
 
 def reduce_blocks(blocks, axis):
     blocks = dict(enumerate(blocks))
     for bit in bits_of(lax.axis_size(axis)):
         for s in sorted((s for s in blocks if s & bit), reverse=True):
-            got = across(blocks.pop(s).astype(BF16), axis, bit)
+            sent = blocks.pop(s).astype(BF16)
+            got = across(sent, axis, bit)
             blocks[s ^ bit] = blocks[s ^ bit].astype(F32) + got.astype(F32)
-    return blocks[0]
+    return blocks[0], sent
 
 
 def on_device(queries, keys, values, residual, targets, lang_ids, lang_scale, out_weight):
@@ -308,6 +313,45 @@
         16,
         "attention",
     )
+    half = width // 2
+    cuts = [slice(0, half), slice(half, width)]
+    bits = bits_of(nh)
+    top = bits[-1]
+    share = {}
+
+    def project(offsets, ranges, after=()):
+        for s in offsets:
+            for c, cut in enumerate(ranges):
+                block = call(
+                    functools.partial(project_kernel, width, s, cut),
+                    pltpu.VMEM(
+                        (all_rows, cut.stop - cut.start), BF16 if s & (top - 1) & 1 else F32
+                    ),
+                    (attended, weight),
+                    8,
+                    "project",
+                    after=after,
+                    flops=PROJECT if after else (0 if s & 1 else SECOND),
+                )
+                share[s, c] = [block]
+
+    def total(addends):
+        if len(addends) == 1 and addends[0].dtype == BF16:
+            return addends[0]
+        return call(sum_kernel, pltpu.VMEM(addends[0].shape, BF16), addends, 4, "sum")
+
+    def reduce_to(base):
+        for bit in bits[:-1]:
+            for s, c in sorted((k for k in share if k[0] & bit and k[0] & top == base), reverse=True):
+                share[s ^ bit, c].append(across(total(share.pop((s, c))), "head", bit))
+
+    upper_half = range(nh - 1, top - 1, -1)
+    firsts = [s for s in upper_half if s & (top - 1) & 1]
+    project(firsts, cuts)
+    project([s for s in upper_half if s not in firsts], cuts)
+    reduce_to(top)
+    sent = [total(share.pop((top, c))) for c in (0, 1)]
+    got = [across(block, "head", top) for block in sent]
     row_scales, gap = call(
         prepare_kernel,
         (f32_rows, f32_rows),
@@ -320,77 +364,52 @@
         ),
         4,
         "prepare",
-        flops=3 << 29,
-    )
-
-    half = width // 2
-    cuts = [slice(0, half), slice(half, width)]
-    bits = bits_of(nh)
-    top = bits[-1]
-    share = {}
-
-    def project(offsets, after=()):
-        for s in offsets:
-            block = call(
-                functools.partial(project_kernel, width, [s]),
-                pltpu.VMEM((all_rows, width), BF16 if s & (top - 1) & 1 else F32),
-                (attended, weight),
-                8,
-                "project",
-                after=after,
-            )
-            share[s] = [block]
-
-    def total(addends, cut, after=()):
-        out = pltpu.VMEM((all_rows, cut.stop - cut.start), BF16)
-        return call(functools.partial(sum_kernel, cut), out, addends, 4, "sum", after=after)
-
-    def reduce_to(base):
-        for bit in bits[:-1]:
-            for s in sorted((s for s in share if s & bit and s & top == base), reverse=True):
-                addends = share.pop(s)
-                whole = total(addends, slice(0, width)) if len(addends) > 1 else addends[0]
-                share[s ^ bit].append(across(whole, "head", bit))
-
-    upper_half = range(nh - 1, top - 1, -1)
-    firsts = [s for s in upper_half if s & (top - 1) & 1]
-    if firsts:
-        project(firsts)
-    project([s for s in upper_half if s not in firsts])
-    reduce_to(top)
-    addends = share.pop(top)
-    sent = [total(addends, cut, (gap,)) for cut in cuts]
-    got = [across(block, "head", top) for block in sent]
-    project(range(top - 1, -1, -1), after=sent)
+        after=sent,
+        flops=PREPARE,
+    )
+    project(range(top - 1, -1, -1), [slice(0, width)], after=sent)
     reduce_to(0)
     blocks = {}
     for c, cut in enumerate(cuts):
         blocks[0, c] = call(
             functools.partial(gradient_kernel, cut),
             pltpu.VMEM((all_rows, half), BF16),
-            (row_scales, gap, got[c], *share[0]),
+            (row_scales, gap, got[c], *share[0, 0]),
             4,
             "gradient",
         )
         blocks[top, c] = across(blocks[0, c], "head", top)
-    for bit in reversed(bits[:-1]):
-        for s, c in sorted(blocks):
-            blocks[s ^ bit, c] = across(blocks[s, c], "head", bit)
-    near = [k for k in sorted(blocks) if k[0] < top]
-    far = [(s, 0) for s in range(top, nh)] + [(s, 1) for s in range(top, nh)]
-    grad = ()
-    for used in (near, far[: top + 1]):
-        places = [(s, c * half, half) for s, c in used]
-        out = call(
-            functools.partial(weighted_kernel, width, places),
+
+    def pass_on(places):
+        for bit in reversed(bits[:-1]):
+            for s, c in [k for k in places if k in blocks]:
+                if (s ^ bit, c) not in blocks:
+                    blocks[s ^ bit, c] = across(blocks[s, c], "head", bit)
+
+    def spread(used, *more):
+        return call(
+            functools.partial(weighted_kernel, width, [(s, c * half, half) for s, c in used]),
             pltpu.VMEM((all_rows, q_width), F32),
-            (weight, *(blocks[k] for k in used), *grad),
+            (weight, *(blocks[k] for k in used), *more),
             8,
             "weighted",
-            flops=1 << 31,
+            flops=SPREAD,
         )
-        grad = (out,)
-    last = far[top + 1 :]
+
+    near = [(s, c) for c in (0, 1) for s in range(top)]
+    far = [[(s, c) for s in range(top, nh)] for c in (0, 1)]
+    pass_on(near)
+    grad = spread([k for k in near if not k[0]])
+    blocks[top, 0], grad = lax.optimization_barrier((blocks[top, 0], grad))
+    pass_on(far[0])
+    if top > 1:
+        grad = spread([k for k in near if k[0]], grad)
+    grad = spread(far[0], grad)
+    blocks[top, 1], grad = lax.optimization_barrier((blocks[top, 1], grad))
+    pass_on(far[1])
+    if far[1][:-1]:
+        grad = spread(far[1][:-1], grad)
+    last = far[1][-1:]
     places = [(s, c * half, half) for s, c in last]
     shares = (
         pltpu.VMEM((all_rows, kv_width), F32),
@@ -401,20 +420,33 @@
             value_gradient_kernel, n, places, rows, kv_local, per_group, width
         ),
         (pltpu.VMEM((all_rows, q_width), BF16), *shares),
-        (weight, low_probs, high_probs, *grad, *(blocks[k] for k in last)),
+        (weight, low_probs, high_probs, grad, *(blocks[k] for k in last)),
         16,
         "value_gradient",
     )
-    grad_queries, *grad_keys = call(
+    low_step, high_step, *grad_keys = call(
         functools.partial(key_gradient_kernel, n, rows, kv_local, per_group),
-        (jax.ShapeDtypeStruct((all_rows, q_width), F32), *shares),
-        (grad_attended, flat_q, low_probs, high_probs, *key_blocks, *value_blocks),
+        (
+            pltpu.VMEM(low_probs.shape, BF16),
+            pltpu.VMEM(high_probs.shape, BF16),
+            *shares,
+        ),
+        (grad_attended, flat_q, low_probs, high_probs, *value_blocks),
         16,
         "key_gradient",
-        flops=1 << 31,
-    )
-    grad_values = reduce_blocks(grad_values, "ctx")
-    grad_keys = reduce_blocks(grad_keys, "ctx")
+        flops=KEYS,
+    )
+    grad_values, _ = reduce_blocks(grad_values, "ctx")
+    grad_keys, sent = reduce_blocks(grad_keys, "ctx")
+    grad_queries = call(
+        functools.partial(query_gradient_kernel, n, rows, kv_local, per_group),
+        jax.ShapeDtypeStruct((all_rows, q_width), F32),
+        (low_step, high_step, *key_blocks),
+        16,
+        "query_gradient",
+        after=[sent],
+        flops=QUERIES,
+    )
     return (
         grad_queries.reshape(2, rows, q_width),
         grad_keys.reshape(2, rows, kv_width),

time: 58.1 us -> 52.4 us (0.902)
  waiting for transfers between devices: 15.4 us -> 7.67 us
  starting transfers between devices: 27 us -> 28.8 us
    ppermute x23 -> x24, waiting for transfers between devices: 15.4 us -> 7.67 us  [across(): return lax.ppermute(block, axis, [(i, i ^ bit) for i in range(count)])]
    ppermute x23 -> x24, starting transfers between devices: 27 us -> 28.8 us  [across(): return lax.ppermute(block, axis, [(i, i ^ bit) for i in range(count)])]
    pallas_call x14 -> x19, Pallas kernels: 9.8 us -> 10 us  [call(): pl.pallas_call(padded, out_shape=out, in_specs=[VMEM] * count + [ANY] * e...]
  transfers between devices with their start and end apart: 23 -> 24, of which waited for: 11 -> 8; matrix products, arithmetic and copies ran while one was open for 1% -> 1% of each run, Pallas kernels for 21% -> 24%
where the time goes in v3:
time: 52.4 us; the launch traced here: 52.3 us
  starting transfers between devices  28.8 us (55%)
  Pallas kernels  13.5 us (26%)
  waiting for transfers between devices  7.67 us (15%)
  other arithmetic  1.39 us (3%)
  between operations  0.93 us (2%)
    ppermute x24, starting transfers between devices, across(): return lax.ppermute(block, axis, [(i, i ^ bit) for i in range(count)])  28.8 us
    pallas_call x19, Pallas kernels, call(): pl.pallas_call(padded, out_shape=out, in_specs=[VMEM] * count + [ANY] * e...  10 us
    ppermute x24, waiting for transfers between devices, across(): return lax.ppermute(block, axis, [(i, i ^ bit) for i in range(count)])  7.67 us
    pallas_call x1, Pallas kernels, on_device(): pl.pallas_call(hold_kernel, out_shape=(pltpu.VMEM(out_weight.shape, BF16)...  3.48 us
    add x2, other arithmetic, reduce_blocks(): blocks[s ^ bit] = blocks[s ^ bit].astype(F32) + got.astype(F32)  1.35 us
  transfers between devices with their start and end apart: 24, of which 8 were waited for; matrix products, arithmetic and copies ran while one was open for 1% of the time, Pallas kernels for 24%

profile of v3, /device:TPU:0, one launch (start us, length us, event | category | flops | bytes accessed | tf_op | source)
XLA Modules:
  0.0 52.3 jit_solution(10151482197581632848)
XLA Ops:
  0.7 4.1 %collective-permute-start = (bf16[128,256]{1,0:T(8,128)(2,1)}, bf16[128,256]{1,0:T(8,128)(2,1)S(1)}, u32[]{:S(2)}, u32[]{:S(2)}) collective-permute-start(bf16[128,256]{1,0:T(8,128)(2,1)} %bitcast.13), channel_id=1, source_target_pairs={{0,8},{4,12},{8,0},{12,4},{1,9},{5,13},{9,1},{13,5},{2,10},{6,14},... | collective-permute-start | bytes 196616 | tf_op jit(solution)/shard_map/ppermute | solution.py:23
  4.8 1.8 %collective-permute-start.1 = (bf16[128,256]{1,0:T(8,128)(2,1)}, bf16[128,256]{1,0:T(8,128)(2,1)S(1)}, u32[]{:S(2)}, u32[]{:S(2)}) collective-permute-start(bf16[128,256]{1,0:T(8,128)(2,1)} %bitcast.14), channel_id=1, source_target_pairs={{0,4},{4,0},{8,12},{12,8},{1,5},{5,1},{9,13},{13,9},{2,6},{6,2},{1... | collective-permute-start | bytes 196616 | tf_op jit(solution)/shard_map/ppermute | solution.py:23
  6.9 3.5 %hold.1 = (bf16[1024,4096]{1,0:T(8,128)(2,1)S(1)}, bf16[64,1024]{1,0:T(8,128)(2,1)S(1)}) custom-call(bf16[1024,4096]{1,0:T(8,128)(2,1)} %w_ref.1, bf16[2,64,1024]{2,1,0:T(8,128)(2,1)} %refs_3_.1), custom_call_target="tpu_custom_call" | custom-call | bytes 16777216 | tf_op jit(solution)/shard_map/hold/pallas_call | solution.py:291
  10.4 1.9 %collective-permute-start.2 = (bf16[128,256]{1,0:T(8,128)(2,1)S(1)}, bf16[128,256]{1,0:T(8,128)(2,1)S(1)}, u32[]{:S(2)}, u32[]{:S(2)}) collective-permute-start(bf16[128,256]{1,0:T(8,128)(2,1)S(1)} %collective-permute-done.refs_3_.refs_4_), channel_id=1, source_target_pairs={{0,4},{4,0},{8,12},{12,8},{1,5},{5,1},{9,13},{13,9},{2,6},{6,2},{1... | collective-permute-start | bytes 196616 | tf_op jit(solution)/shard_map/ppermute | solution.py:23
  12.5 3.9 %collective-permute-start.6 = (bf16[64,1024]{1,0:T(8,128)(2,1)S(1)}, bf16[64,1024]{1,0:T(8,128)(2,1)S(1)}, u32[]{:S(2)}, u32[]{:S(2)}) collective-permute-start(bf16[64,1024]{1,0:T(8,128)(2,1)S(1)} %get-tuple-element.32), channel_id=1, source_target_pairs={{0,12},{4,8},{8,4},{12,0},{1,13},{5,9},{9,5},{13,1},{2,14},{6,10},... | collective-permute-start | bytes 393224 | tf_op jit(solution)/shard_map/ppermute | solution.py:23
  16.5 1.0 %attention.1 = (bf16[128,1024]{1,0:T(8,128)(2,1)S(1)}, f32[2,256,256]{2,1,0:T(8,128)S(1)}, f32[2,512,256]{2,1,0:T(8,128)S(1)}) custom-call(bf16[128,1024]{1,0:T(8,128)(2,1)S(1)} %bitcast.7, bf16[128,256]{1,0:T(8,128)(2,1)S(1)} %bitcast.15, bf16[128,256]{1,0:T(8,128)(2,1)S(1)} %collective-permute-done.1.refs_2_.refs_3_, ...), custom_call_target="tpu_custom_call" | custom-call | tf_op jit(solution)/shard_map/attention/pallas_call | solution.py:56
  19.9 1.6 %collective-permute-start.12 = (bf16[128,512]{1,0:T(8,128)(2,1)S(1)}, bf16[128,512]{1,0:T(8,128)(2,1)S(1)}, u32[]{:S(2)}, u32[]{:S(2)}) collective-permute-start(bf16[128,512]{1,0:T(8,128)(2,1)S(1)} %sum.2.refs_5_.refs_2_), channel_id=1, source_target_pairs={{0,2},{1,3},{2,0},{3,1},{4,6},{5,7},{6,4},{7,5},{8,10},{9,11},{10,... | collective-permute-start | bytes 393224 | tf_op jit(solution)/shard_map/ppermute | solution.py:23
  23.8 2.5 %collective-permute-done.12.refs_2_ = bf16[128,512]{1,0:T(8,128)(2,1)S(1)} collective-permute-done((bf16[128,512]{1,0:T(8,128)(2,1)S(1)}, bf16[128,512]{1,0:T(8,128)(2,1)S(1)}, u32[]{:S(2)}, u32[]{:S(2)}) %collective-permute-start.12) | collective-permute-done | bytes 131104 | tf_op jit(solution)/shard_map/ppermute | solution.py:23
  26.3 1.6 %collective-permute-start.13 = (bf16[128,512]{1,0:T(8,128)(2,1)S(1)}, bf16[128,512]{1,0:T(8,128)(2,1)S(1)}, u32[]{:S(2)}, u32[]{:S(2)}) collective-permute-start(bf16[128,512]{1,0:T(8,128)(2,1)S(1)} %gradient.3.refs_1_), channel_id=1, source_target_pairs={{0,2},{1,3},{2,0},{3,1},{4,6},{5,7},{6,4},{7,5},{8,10},{9,11},{10,... | collective-permute-start | bytes 393224 | tf_op jit(solution)/shard_map/ppermute | solution.py:23
  27.9 1.1 %collective-permute-done.9.refs_2_ = bf16[128,512]{1,0:T(8,128)(2,1)S(1)} collective-permute-done((bf16[128,512]{1,0:T(8,128)(2,1)S(1)}, bf16[128,512]{1,0:T(8,128)(2,1)S(1)}, u32[]{:S(2)}, u32[]{:S(2)}) %collective-permute-start.9) | collective-permute-done | bytes 131104 | tf_op jit(solution)/shard_map/ppermute | solution.py:23
  29.1 1.6 %collective-permute-start.11 = (bf16[128,512]{1,0:T(8,128)(2,1)S(1)}, bf16[128,512]{1,0:T(8,128)(2,1)S(1)}, u32[]{:S(2)}, u32[]{:S(2)}) collective-permute-start(bf16[128,512]{1,0:T(8,128)(2,1)S(1)} %gradient.2.refs_2_), channel_id=1, source_target_pairs={{0,2},{1,3},{2,0},{3,1},{4,6},{5,7},{6,4},{7,5},{8,10},{9,11},{10,... | collective-permute-start | bytes 393224 | tf_op jit(solution)/shard_map/ppermute | solution.py:23
  30.7 0.8 %weighted.4.refs_3_ = f32[128,1024]{1,0:T(8,128)S(1)} custom-call(bf16[1024,4096]{1,0:T(8,128)(2,1)S(1)} %get-tuple-element.28.refs_1_.refs_0_, bf16[128,512]{1,0:T(8,128)(2,1)S(1)} %gradient.3.refs_1_, bf16[128,512]{1,0:T(8,128)(2,1)S(1)} %gradient.2.refs_2_), custom_call_target="tpu_custom_call" | custom-call | flops 2147483648 | tf_op jit(solution)/shard_map/weighted/pallas_call | solution.py:56
  31.7 0.8 %weighted.5.refs_3_ = f32[128,1024]{1,0:T(8,128)S(1)} custom-call(bf16[1024,4096]{1,0:T(8,128)(2,1)S(1)} %get-tuple-element.28.refs_1_.refs_0_, bf16[128,512]{1,0:T(8,128)(2,1)S(1)} %collective-permute-done.15.refs_1_, bf16[128,512]{1,0:T(8,128)(2,1)S(1)} %collective-permute-done.16.refs_2_, f32[128,1024]{1,0:T(8,128)S(1)} %weighted.4.refs_3_), custom_call_target="tpu_custom_call" | custom-call | flops 2147483648 | tf_op jit(solution)/shard_map/weighted/pallas_call | solution.py:56
  32.9 0.8 %weighted.6.refs_2_ = f32[128,1024]{1,0:T(8,128)S(1)} custom-call(bf16[1024,4096]{1,0:T(8,128)(2,1)S(1)} %get-tuple-element.28.refs_1_.refs_0_, bf16[128,512]{1,0:T(8,128)(2,1)S(1)} %collective-permute-done.13.refs_1_, bf16[128,512]{1,0:T(8,128)(2,1)S(1)} %collective-permute-done.14.refs_2_, f32[128,1024]{1,0:T(8,128)S(1)} %weighted.5.refs_3_), custom_call_target="tpu_custom_call" | custom-call | flops 2147483648 | tf_op jit(solution)/shard_map/weighted/pallas_call | solution.py:56
  33.7 1.3 %collective-permute-done.11.refs_1_ = bf16[128,512]{1,0:T(8,128)(2,1)S(1)} collective-permute-done((bf16[128,512]{1,0:T(8,128)(2,1)S(1)}, bf16[128,512]{1,0:T(8,128)(2,1)S(1)}, u32[]{:S(2)}, u32[]{:S(2)}) %collective-permute-start.11) | collective-permute-done | bytes 131104 | tf_op jit(solution)/shard_map/ppermute | solution.py:23
  35.5 0.9 %collective-permute-done.17.refs_4_ = bf16[128,512]{1,0:T(8,128)(2,1)S(1)} collective-permute-done((bf16[128,512]{1,0:T(8,128)(2,1)S(1)}, bf16[128,512]{1,0:T(8,128)(2,1)S(1)}, u32[]{:S(2)}, u32[]{:S(2)}) %collective-permute-start.17) | collective-permute-done | bytes 131104 | tf_op jit(solution)/shard_map/ppermute | solution.py:23
  37.1 0.8 %collective-permute-start.22 = (bf16[128,256]{1,0:T(8,128)(2,1)S(1)}, bf16[128,256]{1,0:T(8,128)(2,1)S(1)}, u32[]{:S(2)}, u32[]{:S(2)}) collective-permute-start(bf16[128,256]{1,0:T(8,128)(2,1)S(1)} %get-tuple-element.50), channel_id=1, source_target_pairs={{0,4},{4,0},{8,12},{12,8},{1,5},{5,1},{9,13},{13,9},{2,6},{6,2},{1... | collective-permute-start | bytes 196616 | tf_op jit(solution)/shard_map/ppermute | solution.py:23
  37.9 1.3 %collective-permute-start.21 = (bf16[128,256]{1,0:T(8,128)(2,1)S(1)}, bf16[128,256]{1,0:T(8,128)(2,1)S(1)}, u32[]{:S(2)}, u32[]{:S(2)}) collective-permute-start(bf16[128,256]{1,0:T(8,128)(2,1)S(1)} %get-tuple-element.48), channel_id=1, source_target_pairs={{0,4},{4,0},{8,12},{12,8},{1,5},{5,1},{9,13},{13,9},{2,6},{6,2},{1... | collective-permute-start | bytes 196616 | tf_op jit(solution)/shard_map/ppermute | solution.py:23
  39.2 1.1 %key_gradient.1 = (bf16[2,256,256]{2,1,0:T(8,128)(2,1)S(1)}, bf16[2,512,256]{2,1,0:T(8,128)(2,1)S(1)}, f32[128,256]{1,0:T(8,128)S(1)}, bf16[128,256]{1,0:T(8,128...) custom-call(bf16[128,1024]{1,0:T(8,128)(2,1)S(1)} %get-tuple-element.40.refs_0_, ...), custom_call_target="tpu_custom_call" | custom-call | flops 2147483648 | tf_op jit(solution)/shard_map/key_gradient/pallas_call | solution.py:56
  41.1 1.3 %collective-permute-start.19 = (bf16[128,256]{1,0:T(8,128)(2,1)S(1)}, bf16[128,256]{1,0:T(8,128)(2,1)S(1)}, u32[]{:S(2)}, u32[]{:S(2)}) collective-permute-start(bf16[128,256]{1,0:T(8,128)(2,1)S(1)} %get-tuple-element.46), channel_id=1, source_target_pairs={{0,4},{4,0},{8,12},{12,8},{1,5},{5,1},{9,13},{13,9},{2,6},{6,2},{1... | collective-permute-start | bytes 196616 | tf_op jit(solution)/shard_map/ppermute | solution.py:23
  42.4 3.4 %collective-permute-start.23 = (bf16[128,256]{1,0:T(8,128)(2,1)S(1)}, bf16[128,256]{1,0:T(8,128)(2,1)S(1)}, u32[]{:S(2)}, u32[]{:S(2)}) collective-permute-start(bf16[128,256]{1,0:T(8,128)(2,1)S(1)} %add_convert_fusion), channel_id=1, source_target_pairs={{0,8},{4,12},{8,0},{12,4},{1,9},{5,13},{9,1},{13,5},{2,10},{6,14},... | collective-permute-start | bytes 196616 | tf_op jit(solution)/shard_map/ppermute | solution.py:23
  45.8 2.8 %collective-permute-start.20 = (bf16[128,256]{1,0:T(8,128)(2,1)S(1)}, bf16[128,256]{1,0:T(8,128)(2,1)S(1)}, u32[]{:S(2)}, u32[]{:S(2)}) collective-permute-start(bf16[128,256]{1,0:T(8,128)(2,1)S(1)} %add_convert_fusion.1.refs_6_), channel_id=1, source_target_pairs={{0,8},{4,12},{8,0},{12,4},{1,9},{5,13},{9,1},{13,5},{2,10},{6,14},... | collective-permute-start | bytes 196616 | tf_op jit(solution)/shard_map/ppermute | solution.py:23
  48.7 1.2 %query_gradient.1 = f32[128,1024]{1,0:T(8,128)} custom-call(bf16[2,256,256]{2,1,0:T(8,128)(2,1)S(1)} %get-tuple-element.41.refs_0_, bf16[2,512,256]{2,1,0:T(8,128)(2,1)S(1)} %get-tuple-element.42.refs_1_, bf16[128,256]{1,0:T(8,128)(2,1)S(1)} %bitcast.16, bf16[128,256]{1,0:T(8,128)(2,1)S(1)} %collective-permute-done.1.refs_2_.refs_3_, ...), custom_call_target="tpu_custom_call" | custom-call | flops 2147483648 | tf_op jit(solution)/shard_map/query_gradient/pallas_call | solution.py:56
  50.6 1.0 %collective-permute-done.20 = bf16[128,256]{1,0:T(8,128)(2,1)S(1)} collective-permute-done((bf16[128,256]{1,0:T(8,128)(2,1)S(1)}, bf16[128,256]{1,0:T(8,128)(2,1)S(1)}, u32[]{:S(2)}, u32[]{:S(2)}) %collective-permute-start.20) | collective-permute-done | bytes 65568 | tf_op jit(solution)/shard_map/ppermute | solution.py:23
  (62 shorter events, 9.3 us)
Async XLA Ops:
  0.7 9.7 %collective-permute-start = (bf16[128,256]{1,0:T(8,128)(2,1)}, bf16[128,256]{1,0:T(8,128)(2,1)S(1)}, u32[]{:S(2)}, u32[]{:S(2)}) collective-permute-start(bf16[128,256]{1,0:T(8,128)(2,1)} %bitcast.13), channel_id=1, source_target_pairs={{0,8},{4,12},{8,0},{12,4},{1,9},{5,13},{9,1},{13,5},{2,10},{6,14},... | collective-permute-start | bytes 196616 | tf_op jit(solution)/shard_map/ppermute | solution.py:23
  4.8 7.5 %collective-permute-start.4 = (bf16[128,256]{1,0:T(8,128)(2,1)}, bf16[128,256]{1,0:T(8,128)(2,1)S(1)}, u32[]{:S(2)}, u32[]{:S(2)}) collective-permute-start(bf16[128,256]{1,0:T(8,128)(2,1)} %bitcast.9), channel_id=1, source_target_pairs={{0,8},{4,12},{8,0},{12,4},{1,9},{5,13},{9,1},{13,5},{2,10},{6,14},... | collective-permute-start | bytes 196616 | tf_op jit(solution)/shard_map/ppermute | solution.py:23
  4.8 11.5 %collective-permute-start.1 = (bf16[128,256]{1,0:T(8,128)(2,1)}, bf16[128,256]{1,0:T(8,128)(2,1)S(1)}, u32[]{:S(2)}, u32[]{:S(2)}) collective-permute-start(bf16[128,256]{1,0:T(8,128)(2,1)} %bitcast.14), channel_id=1, source_target_pairs={{0,4},{4,0},{8,12},{12,8},{1,5},{5,1},{9,13},{13,9},{2,6},{6,2},{1... | collective-permute-start | bytes 196616 | tf_op jit(solution)/shard_map/ppermute | solution.py:23
  6.7 9.6 %collective-permute-start.3 = (bf16[128,256]{1,0:T(8,128)(2,1)}, bf16[128,256]{1,0:T(8,128)(2,1)S(1)}, u32[]{:S(2)}, u32[]{:S(2)}) collective-permute-start(bf16[128,256]{1,0:T(8,128)(2,1)} %bitcast.10), channel_id=1, source_target_pairs={{0,4},{4,0},{8,12},{12,8},{1,5},{5,1},{9,13},{13,9},{2,6},{6,2},{1... | collective-permute-start | bytes 196616 | tf_op jit(solution)/shard_map/ppermute | solution.py:23
  10.4 6.0 %collective-permute-start.2 = (bf16[128,256]{1,0:T(8,128)(2,1)S(1)}, bf16[128,256]{1,0:T(8,128)(2,1)S(1)}, u32[]{:S(2)}, u32[]{:S(2)}) collective-permute-start(bf16[128,256]{1,0:T(8,128)(2,1)S(1)} %collective-permute-done.refs_3_.refs_4_), channel_id=1, source_target_pairs={{0,4},{4,0},{8,12},{12,8},{1,5},{5,1},{9,13},{13,9},{2,6},{6,2},{1... | collective-permute-start | bytes 196616 | tf_op jit(solution)/shard_map/ppermute | solution.py:23
  12.3 4.3 %collective-permute-start.5 = (bf16[128,256]{1,0:T(8,128)(2,1)S(1)}, bf16[128,256]{1,0:T(8,128)(2,1)S(1)}, u32[]{:S(2)}, u32[]{:S(2)}) collective-permute-start(bf16[128,256]{1,0:T(8,128)(2,1)S(1)} %collective-permute-done.4.refs_7_.refs_6_), channel_id=1, source_target_pairs={{0,4},{4,0},{8,12},{12,8},{1,5},{5,1},{9,13},{13,9},{2,6},{6,2},{1... | collective-permute-start | bytes 196616 | tf_op jit(solution)/shard_map/ppermute | solution.py:23
  12.5 10.2 %collective-permute-start.6 = (bf16[64,1024]{1,0:T(8,128)(2,1)S(1)}, bf16[64,1024]{1,0:T(8,128)(2,1)S(1)}, u32[]{:S(2)}, u32[]{:S(2)}) collective-permute-start(bf16[64,1024]{1,0:T(8,128)(2,1)S(1)} %get-tuple-element.32), channel_id=1, source_target_pairs={{0,12},{4,8},{8,4},{12,0},{1,13},{5,9},{9,5},{13,1},{2,14},{6,10},... | collective-permute-start | bytes 393224 | tf_op jit(solution)/shard_map/ppermute | solution.py:23
  18.2 3.2 %collective-permute-start.8 = (bf16[128,512]{1,0:T(8,128)(2,1)S(1)}, bf16[128,512]{1,0:T(8,128)(2,1)S(1)}, u32[]{:S(2)}, u32[]{:S(2)}) collective-permute-start(bf16[128,512]{1,0:T(8,128)(2,1)S(1)} %project.9), channel_id=1, source_target_pairs={{0,1},{1,0},{2,3},{3,2},{4,5},{5,4},{6,7},{7,6},{8,9},{9,8},{10,11... | collective-permute-start | bytes 393224 | tf_op jit(solution)/shard_map/ppermute | solution.py:23
  18.3 1.5 %collective-permute-start.7 = (bf16[128,512]{1,0:T(8,128)(2,1)S(1)}, bf16[128,512]{1,0:T(8,128)(2,1)S(1)}, u32[]{:S(2)}, u32[]{:S(2)}) collective-permute-start(bf16[128,512]{1,0:T(8,128)(2,1)S(1)} %project.7), channel_id=1, source_target_pairs={{0,1},{1,0},{2,3},{3,2},{4,5},{5,4},{6,7},{7,6},{8,9},{9,8},{10,11... | collective-permute-start | bytes 393224 | tf_op jit(solution)/shard_map/ppermute | solution.py:23
  19.9 6.4 %collective-permute-start.12 = (bf16[128,512]{1,0:T(8,128)(2,1)S(1)}, bf16[128,512]{1,0:T(8,128)(2,1)S(1)}, u32[]{:S(2)}, u32[]{:S(2)}) collective-permute-start(bf16[128,512]{1,0:T(8,128)(2,1)S(1)} %sum.2.refs_5_.refs_2_), channel_id=1, source_target_pairs={{0,2},{1,3},{2,0},{3,1},{4,6},{5,7},{6,4},{7,5},{8,10},{9,11},{10,... | collective-permute-start | bytes 393224 | tf_op jit(solution)/shard_map/ppermute | solution.py:23
  21.5 7.5 %collective-permute-start.9 = (bf16[128,512]{1,0:T(8,128)(2,1)S(1)}, bf16[128,512]{1,0:T(8,128)(2,1)S(1)}, u32[]{:S(2)}, u32[]{:S(2)}) collective-permute-start(bf16[128,512]{1,0:T(8,128)(2,1)S(1)} %sum.3.refs_6_.refs_3_), channel_id=1, source_target_pairs={{0,2},{1,3},{2,0},{3,1},{4,6},{5,7},{6,4},{7,5},{8,10},{9,11},{10,... | collective-permute-start | bytes 393224 | tf_op jit(solution)/shard_map/ppermute | solution.py:23
  22.5 3.7 %collective-permute-start.10 = (bf16[128,1024]{1,0:T(8,128)(2,1)S(1)}, bf16[128,1024]{1,0:T(8,128)(2,1)S(1)}, u32[]{:S(2)}, u32[]{:S(2)}) collective-permute-start(bf16[128,1024]{1,0:T(8,128)(2,1)S(1)} %project.11), channel_id=1, source_target_pairs={{0,1},{1,0},{2,3},{3,2},{4,5},{5,4},{6,7},{7,6},{8,9},{9,8},{10,11... | collective-permute-start | bytes 786440 | tf_op jit(solution)/shard_map/ppermute | solution.py:23
  26.3 5.2 %collective-permute-start.13 = (bf16[128,512]{1,0:T(8,128)(2,1)S(1)}, bf16[128,512]{1,0:T(8,128)(2,1)S(1)}, u32[]{:S(2)}, u32[]{:S(2)}) collective-permute-start(bf16[128,512]{1,0:T(8,128)(2,1)S(1)} %gradient.3.refs_1_), channel_id=1, source_target_pairs={{0,2},{1,3},{2,0},{3,1},{4,6},{5,7},{6,4},{7,5},{8,10},{9,11},{10,... | collective-permute-start | bytes 393224 | tf_op jit(solution)/shard_map/ppermute | solution.py:23
  27.9 3.8 %collective-permute-start.15 = (bf16[128,512]{1,0:T(8,128)(2,1)S(1)}, bf16[128,512]{1,0:T(8,128)(2,1)S(1)}, u32[]{:S(2)}, u32[]{:S(2)}) collective-permute-start(bf16[128,512]{1,0:T(8,128)(2,1)S(1)} %gradient.3.refs_1_), channel_id=1, source_target_pairs={{0,1},{1,0},{2,3},{3,2},{4,5},{5,4},{6,7},{7,6},{8,9},{9,8},{10,11... | collective-permute-start | bytes 393224 | tf_op jit(solution)/shard_map/ppermute | solution.py:23
  29.0 2.7 %collective-permute-start.16 = (bf16[128,512]{1,0:T(8,128)(2,1)S(1)}, bf16[128,512]{1,0:T(8,128)(2,1)S(1)}, u32[]{:S(2)}, u32[]{:S(2)}) collective-permute-start(bf16[128,512]{1,0:T(8,128)(2,1)S(1)} %gradient.2.refs_2_), channel_id=1, source_target_pairs={{0,1},{1,0},{2,3},{3,2},{4,5},{5,4},{6,7},{7,6},{8,9},{9,8},{10,11... | collective-permute-start | bytes 393224 | tf_op jit(solution)/shard_map/ppermute | solution.py:23
  29.1 5.9 %collective-permute-start.11 = (bf16[128,512]{1,0:T(8,128)(2,1)S(1)}, bf16[128,512]{1,0:T(8,128)(2,1)S(1)}, u32[]{:S(2)}, u32[]{:S(2)}) collective-permute-start(bf16[128,512]{1,0:T(8,128)(2,1)S(1)} %gradient.2.refs_2_), channel_id=1, source_target_pairs={{0,2},{1,3},{2,0},{3,1},{4,6},{5,7},{6,4},{7,5},{8,10},{9,11},{10,... | collective-permute-start | bytes 393224 | tf_op jit(solution)/shard_map/ppermute | solution.py:23
  31.5 1.4 %collective-permute-start.14 = (bf16[128,512]{1,0:T(8,128)(2,1)S(1)}, bf16[128,512]{1,0:T(8,128)(2,1)S(1)}, u32[]{:S(2)}, u32[]{:S(2)}) collective-permute-start(bf16[128,512]{1,0:T(8,128)(2,1)S(1)} %collective-permute-done.13.refs_1_), channel_id=1, source_target_pairs={{0,1},{1,0},{2,3},{3,2},{4,5},{5,4},{6,7},{7,6},{8,9},{9,8},{10,11... | collective-permute-start | bytes 393224 | tf_op jit(solution)/shard_map/ppermute | solution.py:23
  35.0 1.3 %collective-permute-start.17 = (bf16[128,512]{1,0:T(8,128)(2,1)S(1)}, bf16[128,512]{1,0:T(8,128)(2,1)S(1)}, u32[]{:S(2)}, u32[]{:S(2)}) collective-permute-start(bf16[128,512]{1,0:T(8,128)(2,1)S(1)} %collective-permute-done.11.refs_1_), channel_id=1, source_target_pairs={{0,1},{1,0},{2,3},{3,2},{4,5},{5,4},{6,7},{7,6},{8,9},{9,8},{10,11... | collective-permute-start | bytes 393224 | tf_op jit(solution)/shard_map/ppermute | solution.py:23
  37.1 5.3 %collective-permute-start.22 = (bf16[128,256]{1,0:T(8,128)(2,1)S(1)}, bf16[128,256]{1,0:T(8,128)(2,1)S(1)}, u32[]{:S(2)}, u32[]{:S(2)}) collective-permute-start(bf16[128,256]{1,0:T(8,128)(2,1)S(1)} %get-tuple-element.50), channel_id=1, source_target_pairs={{0,4},{4,0},{8,12},{12,8},{1,5},{5,1},{9,13},{13,9},{2,6},{6,2},{1... | collective-permute-start | bytes 196616 | tf_op jit(solution)/shard_map/ppermute | solution.py:23
  37.9 12.0 %collective-permute-start.21 = (bf16[128,256]{1,0:T(8,128)(2,1)S(1)}, bf16[128,256]{1,0:T(8,128)(2,1)S(1)}, u32[]{:S(2)}, u32[]{:S(2)}) collective-permute-start(bf16[128,256]{1,0:T(8,128)(2,1)S(1)} %get-tuple-element.48), channel_id=1, source_target_pairs={{0,4},{4,0},{8,12},{12,8},{1,5},{5,1},{9,13},{13,9},{2,6},{6,2},{1... | collective-permute-start | bytes 196616 | tf_op jit(solution)/shard_map/ppermute | solution.py:23
  40.3 5.5 %collective-permute-start.18 = (bf16[128,256]{1,0:T(8,128)(2,1)S(1)}, bf16[128,256]{1,0:T(8,128)(2,1)S(1)}, u32[]{:S(2)}, u32[]{:S(2)}) collective-permute-start(bf16[128,256]{1,0:T(8,128)(2,1)S(1)} %get-tuple-element.44), channel_id=1, source_target_pairs={{0,4},{4,0},{8,12},{12,8},{1,5},{5,1},{9,13},{13,9},{2,6},{6,2},{1... | collective-permute-start | bytes 196616 | tf_op jit(solution)/shard_map/ppermute | solution.py:23
  41.1 9.5 %collective-permute-start.19 = (bf16[128,256]{1,0:T(8,128)(2,1)S(1)}, bf16[128,256]{1,0:T(8,128)(2,1)S(1)}, u32[]{:S(2)}, u32[]{:S(2)}) collective-permute-start(bf16[128,256]{1,0:T(8,128)(2,1)S(1)} %get-tuple-element.46), channel_id=1, source_target_pairs={{0,4},{4,0},{8,12},{12,8},{1,5},{5,1},{9,13},{13,9},{2,6},{6,2},{1... | collective-permute-start | bytes 196616 | tf_op jit(solution)/shard_map/ppermute | solution.py:23
  42.4 7.4 %collective-permute-start.23 = (bf16[128,256]{1,0:T(8,128)(2,1)S(1)}, bf16[128,256]{1,0:T(8,128)(2,1)S(1)}, u32[]{:S(2)}, u32[]{:S(2)}) collective-permute-start(bf16[128,256]{1,0:T(8,128)(2,1)S(1)} %add_convert_fusion), channel_id=1, source_target_pairs={{0,8},{4,12},{8,0},{12,4},{1,9},{5,13},{9,1},{13,5},{2,10},{6,14},... | collective-permute-start | bytes 196616 | tf_op jit(solution)/shard_map/ppermute | solution.py:23
  45.8 5.8 %collective-permute-start.20 = (bf16[128,256]{1,0:T(8,128)(2,1)S(1)}, bf16[128,256]{1,0:T(8,128)(2,1)S(1)}, u32[]{:S(2)}, u32[]{:S(2)}) collective-permute-start(bf16[128,256]{1,0:T(8,128)(2,1)S(1)} %add_convert_fusion.1.refs_6_), channel_id=1, source_target_pairs={{0,8},{4,12},{8,0},{12,4},{1,9},{5,13},{9,1},{13,5},{2,10},{6,14},... | collective-permute-start | bytes 196616 | tf_op jit(solution)/shard_map/ppermute | solution.py:23
  (7 other events, 61.6 us)
